TPU v7x, 256 devices: a whole 4x4x8 slice. The times are simulated.
256 devices in a mesh: wide: 64 (over y_hi, z, x), narrow: 4 (over y_lo, core).
Axes of the slice: x: 4, y: 4 (y_hi: 2, y_lo: 2; y = y_hi * 2 + y_lo), z: 8, core: 2. Of those that a mesh axis runs over, the one named last changes fastest.
Arguments:
- image_feats: bfloat16 [12288, 1152], P(('wide', 'narrow')), may hold values from -400 to 400
- proj_weight: bfloat16 [1152, 1152], replicated, may hold values from -0.1875 to 0.1875
- text_embed: bfloat16 [12288, 1152], P(('wide', 'narrow')), may hold values from -400 to 400
- log_scale: float32 [1], replicated, may hold values from 1.6 to 2.4
- logit_bias: float32 [1], replicated, may hold values from -7 to -4
Outputs:
- image_loss: float32 [12288], P(('wide', 'narrow'))
- d_text_unit: float32 [12288, 1152], P(('wide', 'narrow'))
- d_proj: float32 [1152, 1152], P('wide', 'narrow')
All inputs are finite; a program needn't handle non-finite values.
Results may differ from a plain program's by a relative error of at most 0.0037.
Values may be sent and summed in bfloat16 or wider, within the bound.
A program may use at most 64 MiB of HBM per device.

v0:
```python
import jax
import jax.numpy as jnp
from jax import lax
from jax.sharding import PartitionSpec as P


def passed_along(value, axis, steps):
    count = lax.axis_size(axis)
    pairs = [(source, (source + steps) % count) for source in range(count)]
    return lax.ppermute(value, axis, pairs)


def unit_rows(values):
    inverse = lax.rsqrt(jnp.sum(values * values, axis=1, keepdims=True) + 1e-06)
    return (values * inverse, inverse)


def pair_terms(group_img, captions, own_pair, logit_scale, logit_shift):
    products = lax.dot_general(
        group_img, captions, (((1,), (1,)), ((), ())), preferred_element_type=jnp.float32
    )
    logits = logit_scale * products + logit_shift
    label_sign = jnp.where(own_pair, 1.0, -1.0).astype(jnp.float32)
    loss_rows = jnp.sum(jax.nn.softplus(-label_sign * logits), axis=1)
    grad_tile = (-logit_scale * label_sign * jax.nn.sigmoid(-label_sign * logits)).astype(
        jnp.bfloat16
    )
    return (loss_rows, grad_tile)


def transposed_product(grad_tile, group_img):
    return lax.dot_general(
        grad_tile, group_img, (((0,), (0,)), ((), ())), preferred_element_type=jnp.float32
    )


def local(image_feats, proj_weight, text_embed, log_scale, logit_bias):
    row_count = image_feats.shape[0]
    width = image_feats.shape[1]
    wide_count = lax.axis_size("wide")
    narrow_pos = lax.axis_index("narrow")
    zproj = jnp.dot(image_feats, proj_weight, preferred_element_type=jnp.float32)
    img_unit, img_inv = unit_rows(zproj)
    group_img = lax.all_gather(img_unit.astype(jnp.bfloat16), "narrow", axis=0, tiled=True)
    group_rows = group_img.shape[0]
    txt_unit, txt_inv = unit_rows(text_embed.astype(jnp.float32))
    txt_emb = txt_unit.astype(jnp.bfloat16)
    logit_scale = jnp.exp(log_scale[0])
    logit_shift = logit_bias[0]
    image_idx = lax.broadcasted_iota(jnp.int32, (group_rows, row_count), 0)
    caption_idx = lax.broadcasted_iota(jnp.int32, (group_rows, row_count), 1)
    diagonal = image_idx == narrow_pos * row_count + caption_idx

    def cycle_step(cycle_pos, state):
        caption_block, caption_grad, d_img, loss_total = state
        own_pair = jnp.logical_and(diagonal, cycle_pos == 0)
        loss_rows, grad_tile = pair_terms(
            group_img, caption_block, own_pair, logit_scale, logit_shift
        )
        d_img = d_img + jnp.dot(grad_tile, caption_block, preferred_element_type=jnp.float32)
        caption_grad = caption_grad + transposed_product(grad_tile, group_img)
        caption_block = passed_along(caption_block, "wide", 1)
        caption_grad = passed_along(caption_grad, "wide", 1)
        return (caption_block, caption_grad, d_img, loss_total + loss_rows)

    start_state = (
        txt_emb,
        jnp.zeros((row_count, width), jnp.float32),
        jnp.zeros((group_rows, width), jnp.float32),
        jnp.zeros((group_rows,), jnp.float32),
    )
    caption_block, caption_grad, d_img, loss_total = lax.fori_loop(
        0, wide_count - 1, cycle_step, start_state
    )
    last_pair = jnp.logical_and(diagonal, wide_count == 1)
    loss_rows, grad_tile = pair_terms(group_img, caption_block, last_pair, logit_scale, logit_shift)
    d_img = d_img + jnp.dot(grad_tile, caption_block, preferred_element_type=jnp.float32)
    caption_grad = caption_grad + transposed_product(grad_tile, group_img)
    loss_total = loss_total + loss_rows
    d_text_unit = passed_along(caption_grad, "wide", 1)
    img_grad, image_loss = (
        lax.psum_scatter(d_img, "narrow", scatter_dimension=0, tiled=True),
        lax.psum_scatter(loss_total, "narrow", scatter_dimension=0, tiled=True),
    )
    d_zproj = (
        img_inv * (img_grad - img_unit * jnp.sum(img_unit * img_grad, axis=1, keepdims=True))
    ).astype(jnp.bfloat16)
    shard_rows = lax.psum_scatter(
        transposed_product(image_feats, d_zproj), "wide", scatter_dimension=0, tiled=True
    )
    d_proj = lax.psum_scatter(shard_rows, "narrow", scatter_dimension=1, tiled=True)
    return (image_loss, d_text_unit, d_proj)


def solution(mesh):
    placed = (P(("wide", "narrow"), None), P(), P(("wide", "narrow"), None), P(), P())
    return jax.shard_map(
        local,
        mesh=mesh,
        in_specs=placed,
        out_specs=(P(("wide", "narrow")), P(("wide", "narrow"), None), P("wide", "narrow")),
        check_vma=False,
    )
```

profile of v0, /device:TPU:1, one launch (start us, length us, event | category | flops | bytes accessed | tf_op | source)
XLA Modules:
  0.0 1895.5 jit_solution(9476255527673802085)
XLA Ops:
  13.8 9.8 all_gather.3
  24.3 1106.7 %while.21 = (s32[]{:T(128)}, bf16[48,1152]{1,0:T(8,128)(2,1)}, f32[48,1152]{1,0:T(8,128)}, f32[192,1152]{1,0:T(8,128)S(1)}, f32[192]{0:T(256)S(1)}, /*index=5*/f...) while((s32[]{:T(128)}, bf16[48,1152]{1,0:T(8,128)(2,1)}, ...), condition=%wide.region_4.5_spmd.clone, body=%wide.region_2.4_spmd.clone.sunk | while | flops 64493760 | bytes 4980514 | solution.py:72
  38.3 6.4 collective-permute-done.1
  55.9 6.7 collective-permute-done.1
  124.7 6.4 collective-permute-done.1
  142.3 6.4 collective-permute-done.1
  159.8 6.4 collective-permute-done.1
  177.4 6.4 collective-permute-done.1
  194.9 6.4 collective-permute-done.1
  212.5 6.4 collective-permute-done.1
  230.0 6.4 collective-permute-done.1
  247.5 6.4 collective-permute-done.1
  265.1 6.4 collective-permute-done.1
  282.6 6.4 collective-permute-done.1
  300.2 6.4 collective-permute-done.1
  317.7 6.4 collective-permute-done.1
  335.2 6.4 collective-permute-done.1
  352.8 6.4 collective-permute-done.1
  370.3 6.4 collective-permute-done.1
  387.9 6.4 collective-permute-done.1
  405.4 6.4 collective-permute-done.1
  422.9 6.4 collective-permute-done.1
  440.5 6.4 collective-permute-done.1
  458.0 6.4 collective-permute-done.1
  475.6 6.4 collective-permute-done.1
  493.1 6.4 collective-permute-done.1
  510.7 6.4 collective-permute-done.1
  528.2 6.4 collective-permute-done.1
  545.7 6.4 collective-permute-done.1
  563.3 6.4 collective-permute-done.1
  580.8 6.4 collective-permute-done.1
  598.4 6.4 collective-permute-done.1
  615.9 6.4 collective-permute-done.1
  633.4 6.4 collective-permute-done.1
  651.0 6.4 collective-permute-done.1
  668.5 6.4 collective-permute-done.1
  686.1 6.4 collective-permute-done.1
  703.6 6.4 collective-permute-done.1
  721.1 6.4 collective-permute-done.1
  738.7 6.4 collective-permute-done.1
  756.2 6.4 collective-permute-done.1
  773.8 6.4 collective-permute-done.1
  791.3 6.4 collective-permute-done.1
  808.8 6.4 collective-permute-done.1
  826.4 6.4 collective-permute-done.1
  843.9 6.4 collective-permute-done.1
  861.5 6.4 collective-permute-done.1
  879.0 6.4 collective-permute-done.1
  896.6 6.4 collective-permute-done.1
  914.1 6.4 collective-permute-done.1
  931.6 6.4 collective-permute-done.1
  949.2 6.4 collective-permute-done.1
  966.7 6.4 collective-permute-done.1
  984.3 6.4 collective-permute-done.1
  1001.8 6.4 collective-permute-done.1
  1019.3 6.4 collective-permute-done.1
  1036.9 6.4 collective-permute-done.1
  1054.4 6.4 collective-permute-done.1
  1089.5 6.4 collective-permute-done.1
  1124.6 6.4 collective-permute-done.1
  1135.1 18.5 reduce-scatter.4.cloned.1.call-done
  1163.1 660.0 %all-reduce.4.cloned.1.call-done = f32[1152,1152]{0,1:T(8,128)} async-done(((f32[1152,1152]{0,1:T(8,128)}), f32[1152,1152]{0,1:T(8,128)}) %all-reduce.4.cloned.1.call-update) | async-done | bytes 5308432
  1826.7 48.2 %all-reduce = f32[192]{0:T(256)S(1)} all-reduce(f32[192]{0:T(256)S(1)} %add.134), channel_id=2, replica_groups=mesh['wide'=64,'narrow'=4] {'narrow'}, use_global_device_ids=true, to_apply=%region_6.7.clone | all-reduce | flops 192 | bytes 1536
  1875.5 11.2 reduce-scatter.6.cloned.1.call-done
  (553 shorter events, 760.6 us)
Async XLA Ops:
  7.2 1146.4 %reduce-scatter.4.cloned.1.call-start = ((), (), s32[]{:S(2)}) async-start(), calls=%async_computation.2 | async-start | bytes 1105920 | tf_op jit(solution)/shard_map/reduce_scatter | solution.py:82
  25.8 12.5 collective-permute-start
  29.9 14.9 collective-permute-start.1
  50.3 12.3 collective-permute-start.1
  119.1 12.0 collective-permute-start.1
  136.7 12.0 collective-permute-start.1
  154.2 12.0 collective-permute-start.1
  171.8 12.0 collective-permute-start.1
  189.3 12.0 collective-permute-start.1
  206.8 12.0 collective-permute-start.1
  224.4 12.0 collective-permute-start.1
  241.9 12.0 collective-permute-start.1
  259.5 12.0 collective-permute-start.1
  277.0 12.0 collective-permute-start.1
  294.6 12.0 collective-permute-start.1
  312.1 12.0 collective-permute-start.1
  329.6 12.0 collective-permute-start.1
  347.2 12.0 collective-permute-start.1
  364.7 12.0 collective-permute-start.1
  382.3 12.0 collective-permute-start.1
  399.8 12.0 collective-permute-start.1
  417.3 12.0 collective-permute-start.1
  434.9 12.0 collective-permute-start.1
  452.4 12.0 collective-permute-start.1
  470.0 12.0 collective-permute-start.1
  487.5 12.0 collective-permute-start.1
  505.0 12.0 collective-permute-start.1
  522.6 12.0 collective-permute-start.1
  540.1 12.0 collective-permute-start.1
  557.7 12.0 collective-permute-start.1
  575.2 12.0 collective-permute-start.1
  592.7 12.0 collective-permute-start.1
  610.3 12.0 collective-permute-start.1
  627.8 12.0 collective-permute-start.1
  645.4 12.0 collective-permute-start.1
  662.9 12.0 collective-permute-start.1
  680.5 12.0 collective-permute-start.1
  698.0 12.0 collective-permute-start.1
  715.5 12.0 collective-permute-start.1
  733.1 12.0 collective-permute-start.1
  750.6 12.0 collective-permute-start.1
  768.2 12.0 collective-permute-start.1
  785.7 12.0 collective-permute-start.1
  803.2 12.0 collective-permute-start.1
  820.8 12.0 collective-permute-start.1
  838.3 12.0 collective-permute-start.1
  855.9 12.0 collective-permute-start.1
  873.4 12.0 collective-permute-start.1
  890.9 12.0 collective-permute-start.1
  908.5 12.0 collective-permute-start.1
  926.0 12.0 collective-permute-start.1
  943.6 12.0 collective-permute-start.1
  961.1 12.0 collective-permute-start.1
  978.7 12.0 collective-permute-start.1
  996.2 12.0 collective-permute-start.1
  1013.7 12.0 collective-permute-start.1
  1031.3 12.0 collective-permute-start.1
  1066.4 12.0 collective-permute-start.1
  1083.9 12.0 collective-permute-start.1
  1101.4 12.0 collective-permute-start.1
  1119.0 12.0 collective-permute-start.1
  1135.1 688.0 %all-reduce.4.cloned.1.call-start = ((), (), s32[]{:S(2)}) async-start(), calls=%async_computation.4 | async-start | bytes 10616832
  1159.4 727.3 %reduce-scatter.6.cloned.1.call-start = ((), (), s32[]{:S(2)}) async-start(), calls=%async_computation.3 | async-start | bytes 737280 | tf_op jit(solution)/shard_map/reduce_scatter | solution.py:91
  1160.6 714.9 %collective-permute-start.2 = (f32[48,1152]{1,0:T(8,128)S(1)}, f32[48,1152]{1,0:T(8,128)S(1)}, u32[]{:S(2)}, u32[]{:S(2)}) collective-permute-start(f32[48,1152]{1,0:T(8,128)S(1)} %convolution_add_fusion.3), channel_id=1, source_target_pairs={{0,4},{4,8},{8,12},{12,16},{16,20},{20,24},{24,28},{28,32},{32,36}... | collective-permute-start | bytes 663560 | tf_op jit(solution)/shard_map/ppermute | solution.py:10
  (73 other events, 1331.6 us)
Sparse Core Ops, SparseCore 0:
  1135.2 18.3 reduce-scatter.3
  1159.5 663.5 all-reduce.3
  1825.6 61.0 reduce-scatter.5
where the time goes:
time: 1900 us
  waiting for transfers between devices  1350 us (71%)
  matrix products  359 us (19%)
  local copies, waits for them, and re-layouts  105 us (6%)
  blocking collectives  58 us (3%)
    unnamed x4, waiting for transfers between devices  660 us
    ppermute x127, waiting for transfers between devices, passed_along(): return lax.ppermute(value, axis, pairs)  659 us
    dot_general x65, matrix products, transposed_product(): lax.dot_general(grad_tile, group_img, (((0,), (0,)), ((), ())), preferred...  133 us
    dot_general x64, matrix products, pair_terms(): lax.dot_general(group_img, captions, (((1,), (1,)), ((), ())), preferred_...  128 us
    while x63, local copies, waits for them, and re-layouts  96.9 us
    dot_general x63, matrix products, cycle_step(): jnp.dot(grad_tile, caption_block, preferred_element_type=jnp.float32)  94.2 us
    unnamed x1, blocking collectives  48.2 us
  transfers between devices with their start and end apart: 130, of which 129 were waited for; matrix products, arithmetic and copies ran while one was open for 19% of the time, Pallas kernels for 0%

commit v1 on v0

v1 whole, which is shorter than its diff:
```python
import functools

import jax
import jax.numpy as jnp
from jax import lax
from jax.experimental import pallas as pl
from jax.experimental.pallas import tpu as pltpu
from jax.sharding import PartitionSpec as P

MESH = pl.DeviceIdType.MESH
F32 = jnp.float32
BF16 = jnp.bfloat16

NX, NY, NZ = 4, 4, 8
STREAM = ("L4", "L3", "S3", "L2", "S2", "L1", "S1", "0")
SLOTS = (
    ("X", "L4"), ("X", "L3"), ("X", "S3"), ("O", "L4"), ("O", "L3"), ("O", "S3"),
    ("X", "L2"), ("X", "S2"), ("O", "L2"), ("O", "S2"),
    ("X", "L1"), ("X", "S1"), ("X", "0"), ("O", "L1"), ("O", "S1"), ("O", "0"),
)
SLOT_ROW = {name: i for i, name in enumerate(SLOTS)}
BATCHES = ((0, 6), (6, 10), (10, 16))
RING = STREAM[:7]
ROW_OF_DQ = {2: 0, 1: 1, 0: 2, 3: 3}


def kernel(
    scale_ref, shift_ref, feats_ref, w_hbm, text_ref,
    loss_out, dtext_out, dproj_out,
    wv, ua, fa, za, ta, g, unit, inv, dimg, lossp, psend, precv, rsend, rrecv,
    dtx, hsend, hrecv, qsend, qrecv, tsend, trecv, fsel, pf, pb, precvb, fin,
    w_sem, a_ring_send, a_ring_recv, a_part_send, a_part_recv,
    b_send, b_recv, ps_sem, pr_sem, rs_sem, rr_sem,
    hs_sem, hr_sem, qs_sem, qr_sem, ts_sem, tr_sem, fs_sem, fr_sem,
):
    rows, width = feats_ref.shape
    chunk = 16
    n_chunk = rows // chunk
    wide = lax.axis_index("wide")
    narrow = lax.axis_index("narrow")
    x = wide % NX
    z = (wide // NX) % NZ
    y = (wide // (NX * NZ)) * 2 + narrow // 2
    core = narrow % 2

    def dev(dx=0, dy=0, dz=0, other=False):
        tx = (x + dx) % NX
        ty = (y + dy) % NY
        tz = (z + dz) % NZ
        tc = (1 - core) if other else core
        return ((ty // 2) * (NX * NZ) + tz * NX + tx, (ty % 2) * 2 + tc)

    def dev_b(dp, dq):
        return dev(dx=dp * (1 - core) + dq * core, dy=dp * core + dq * (1 - core))

    step_z = 1 + core * (NZ - 2)
    along = dev(dz=step_z)
    against = dev(dz=NZ - step_z)
    partner = dev(other=True)

    def rcopy(src, dst, ssem, rsem, target):
        return pltpu.make_async_remote_copy(
            src_ref=src, dst_ref=dst, send_sem=ssem, recv_sem=rsem,
            device_id=target, device_id_type=MESH,
        )

    sends = []

    def send(src, dst, ssem, rsem, target):
        copy = rcopy(src, dst, ssem, rsem, target)
        copy.start()
        sends.append(copy)

    def arrived(dst, ssem, rsem, target):
        rcopy(dst, dst, ssem, rsem, target).wait_recv()

    barrier = pltpu.get_barrier_semaphore()
    peers = [dev_b(dp, dq) for dp in range(4) for dq in range(4) if (dp, dq) != (0, 0)]
    peers += [along, against, partner]
    for peer in peers:
        pl.semaphore_signal(barrier, inc=1, device_id=peer, device_id_type=MESH)
    w_copy = pltpu.make_async_copy(w_hbm, wv, w_sem)
    w_copy.start()

    def part(buf, slot, c):
        return buf.at[pl.ds(SLOT_ROW[slot] * rows + c * chunk, chunk)]

    def a_copy(k, buf, name, c, to_name, target):
        i = STREAM.index(to_name)
        send(
            part(buf, ("O", name), c), part(buf, ("O", to_name), c),
            a_ring_send.at[k, i, c], a_ring_recv.at[k, i, c], target,
        )

    def a_hand(k, buf, name, c):
        i = STREAM.index(name)
        send(
            part(buf, ("O", name), c), part(buf, ("X", name), c),
            a_part_send.at[k, i, c], a_part_recv.at[k, i, c], partner,
        )

    def a_start(k, buf):
        for c in range(n_chunk):
            a_copy(k, buf, "0", c, "L1", along)
            a_copy(k, buf, "0", c, "S1", against)
            a_hand(k, buf, "0", c)

    def a_wait(k, buf, name, c):
        i = STREAM.index(name)
        arrived(part(buf, ("O", name), c), a_ring_send.at[k, i, c], a_ring_recv.at[k, i, c], along)

    def a_step(k, buf, n):
        for c in range(n_chunk):
            a_wait(k, buf, f"L{n}", c)
            if n < 4:
                a_copy(k, buf, f"L{n}", c, f"L{n + 1}", along)
            a_hand(k, buf, f"L{n}", c)
            if n <= 3:
                a_wait(k, buf, f"S{n}", c)
                if n < 3:
                    a_copy(k, buf, f"S{n}", c, f"S{n + 1}", against)
                a_hand(k, buf, f"S{n}", c)

    def a_finish(k, buf):
        for name in STREAM:
            i = STREAM.index(name)
            for c in range(n_chunk):
                arrived(part(buf, ("X", name), c), a_part_send.at[k, i, c], a_part_recv.at[k, i, c], partner)

    def t_slot(dp, dq):
        return ta.at[pl.ds((ROW_OF_DQ[dq % 4] * 4 + dp % 4) * rows, rows)]

    def b_copy(dp, dq, mp, mq):
        to = ((dp - mp) % 4, (dq - mq) % 4)
        send(
            t_slot(dp, dq), t_slot(*to), b_send.at[to[1] * 4 + to[0]], b_recv.at[to[1] * 4 + to[0]],
            dev_b(mp % 4, mq % 4),
        )

    def b_wait(dp, dq):
        i = dq * 4 + dp
        arrived(t_slot(dp, dq), b_send.at[i], b_recv.at[i], partner)

    def b_spread(dp):
        b_copy(dp, 0, 0, 1)
        b_copy(dp, 0, 0, -1)

    text = text_ref[...].astype(F32)
    text_inv = lax.rsqrt(jnp.sum(text * text, axis=1, keepdims=True) + 1e-06)
    own_t = ROW_OF_DQ[0] * 4 * rows
    ta[own_t : own_t + rows] = (text * text_inv).astype(BF16)
    own_u = SLOT_ROW[("O", "0")] * rows
    fa[own_u : own_u + rows] = feats_ref[...]

    pl.semaphore_wait(barrier, len(peers))
    b_copy(0, 0, 1, 0)
    b_copy(0, 0, -1, 0)
    b_spread(0)

    w_copy.wait()
    zproj = jnp.dot(feats_ref[...], wv[...], preferred_element_type=F32)
    img_inv = lax.rsqrt(jnp.sum(zproj * zproj, axis=1, keepdims=True) + 1e-06)
    img_unit = zproj * img_inv
    unit[...] = img_unit
    inv[...] = jnp.broadcast_to(img_inv, inv.shape)
    ua[own_u : own_u + rows] = img_unit.astype(BF16)
    a_start(0, ua)

    b_wait(3, 0)
    b_copy(3, 0, 1, 0)
    b_spread(3)
    b_wait(1, 0)
    b_spread(1)
    a_step(0, ua, 1)
    b_wait(2, 0)
    b_spread(2)
    for dp in (0, 2):
        b_wait(dp, 3)
        b_copy(dp, 3, 0, 1)
    for dp in (3, 1):
        b_wait(dp, 1)
        b_copy(dp, 1, 0, -1)
    a_step(0, ua, 2)
    a_step(0, ua, 3)
    a_start(1, fa)
    a_step(0, ua, 4)
    for dp in (0, 2):
        b_wait(dp, 1)
    for dp in (3, 1):
        b_wait(dp, 3)
    for dp in range(4):
        b_wait(dp, 2)
    a_finish(0, ua)
    a_step(1, fa, 1)

    scale = jnp.exp(jnp.full((1, 128), scale_ref[0], F32))[:, :1]
    shift = shift_ref[0]
    lossp[...] = jnp.zeros_like(lossp)
    half = 8 * rows
    tile = 256

    def pairs(i, carry):
        pair = i // 3
        r0 = pl.multiple_of((i % 3) * tile, tile)
        t0 = pl.multiple_of(pair * half, 16)
        prod = lax.dot_general(
            ua[pl.ds(r0, tile), :], ta[pl.ds(t0, half), :], (((1,), (1,)), ((), ())),
            preferred_element_type=F32,
        )
        total = None
        for j in range(half // 128):
            logit = scale * prod[:, 128 * j : 128 * (j + 1)] + shift
            factor = scale
            if j == 0:
                row = lax.broadcasted_iota(jnp.int32, logit.shape, 0) + (r0 - own_u)
                col = lax.broadcasted_iota(jnp.int32, logit.shape, 1)
                own = jnp.logical_and(row == col, pair == 1)
                logit = jnp.where(own, -logit, logit)
                factor = jnp.where(own, -scale, scale)
            e = jnp.exp(logit)
            g[pair, pl.ds(r0, tile), 128 * j : 128 * (j + 1)] = (factor * (e / (1.0 + e))).astype(BF16)
            term = jnp.log1p(e)
            total = term if total is None else total + term
        lossp[pl.ds(r0, tile), :] += total
        return carry

    lax.fori_loop(0, 6, pairs, 0)
    a_step(1, fa, 2)

    lane = lax.broadcasted_iota(jnp.int32, (rows, 128), 1)

    def slot_rows(slot):
        return pl.ds(SLOT_ROW[slot] * rows, rows)

    def pack(ref, i, value, loss):
        hi = loss.astype(BF16).astype(F32)
        lo = loss - hi
        ref[i, :, :width] = value.astype(BF16)
        ref[i, :, width:] = jnp.where(lane == 0, hi, jnp.where(lane == 1, lo, 0.0)).astype(BF16)

    def unpack(ref, i):
        tail = ref[i, :, width:].astype(F32)
        return ref[i, :, :width].astype(F32), jnp.sum(tail, axis=1, keepdims=True)

    def own_part(slot):
        return dimg[slot_rows(slot), :], jnp.sum(lossp[slot_rows(slot), :], axis=1, keepdims=True)

    def image_batch(b):
        lo, hi = BATCHES[b]
        r = slice(lo * rows, hi * rows)
        acc = jnp.dot(g[0, r, :], ta[:half], preferred_element_type=F32)
        acc += jnp.dot(g[1, r, :], ta[half:], preferred_element_type=F32)
        dimg[r, :] = acc
        for kind, name in SLOTS[lo:hi]:
            if kind == "X":
                i = STREAM.index(name)
                pack(psend, i, *own_part((kind, name)))
                send(psend.at[i], precv.at[i], ps_sem.at[i], pr_sem.at[i], partner)

    def gathered(name):
        i = STREAM.index(name)
        arrived(precv.at[i], ps_sem.at[i], pr_sem.at[i], partner)
        value, loss = own_part(("O", name))
        more, more_loss = unpack(precv, i)
        value, loss = value + more, loss + more_loss
        if name == "0":
            before = ["L1", "S1"]
        elif name in ("L4", "S3"):
            before = []
        else:
            before = [name[0] + str(int(name[1]) + 1)]
        for prev in before:
            j = RING.index(prev)
            arrived(rrecv.at[j], rs_sem.at[j], rr_sem.at[j], along)
            more, more_loss = unpack(rrecv, j)
            value, loss = value + more, loss + more_loss
        return value, loss

    def ring(name):
        i = RING.index(name)
        pack(rsend, i, *gathered(name))
        send(rsend.at[i], rrecv.at[i], rs_sem.at[i], rr_sem.at[i], against if name[0] == "L" else along)

    def caption_half(k):
        dtx[k * half : (k + 1) * half, :] = lax.dot_general(
            g[k], ua[...], (((0,), (0,)), ((), ())), preferred_element_type=F32
        )

    quarter = 4 * rows
    image_batch(0)
    image_batch(1)
    ring("L4")
    ring("S3")
    a_step(1, fa, 3)
    image_batch(2)
    ring("L3")
    caption_half(0)
    hsend[...] = dtx[:quarter].astype(BF16)
    send(hsend.at[: quarter // 2], hrecv.at[0], hs_sem.at[0], hr_sem.at[0], dev_b(0, 1))
    send(hsend.at[quarter // 2 :], hrecv.at[1], hs_sem.at[1], hr_sem.at[1], dev_b(0, 3))
    ring("L2")
    ring("S2")
    a_step(1, fa, 4)
    caption_half(1)

    arrived(hrecv.at[0], hs_sem.at[0], hr_sem.at[0], partner)
    h = quarter // 2
    up, down = quarter, 3 * quarter
    qsend[0, :h] = (dtx[up : up + h] + hrecv[0].astype(F32)).astype(BF16)
    qsend[0, h:] = dtx[up + h : up + quarter].astype(BF16)
    send(qsend.at[0], qrecv.at[0], qs_sem.at[0], qr_sem.at[0], dev_b(0, 1))
    arrived(hrecv.at[1], hs_sem.at[1], hr_sem.at[1], partner)
    qsend[1, :h] = dtx[down : down + h].astype(BF16)
    qsend[1, h:] = (dtx[down + h : down + quarter] + hrecv[1].astype(F32)).astype(BF16)
    send(qsend.at[1], qrecv.at[1], qs_sem.at[1], qr_sem.at[1], dev_b(0, 3))

    ring("L1")
    ring("S1")
    a_finish(1, fa)
    pick_row = lax.broadcasted_iota(jnp.int32, (width, 256), 0)
    pick_col = lax.broadcasted_iota(jnp.int32, (width, 256), 1)
    combo = pick_col >> 5
    inner = pick_col & 31
    wanted = 18 * (32 * (combo >> 2) + 4 * z + (combo & 3)) + inner
    pick = jnp.where(jnp.logical_and(pick_row == wanted, inner < 18), 1.0, 0.0).astype(BF16)
    fsel[...] = jnp.dot(fa[...], pick, preferred_element_type=F32).astype(BF16)

    value, loss = gathered("0")
    loss_out[...] = jnp.broadcast_to(loss, loss_out.shape)
    u = unit[...]
    dz = inv[:, :1] * (value - u * jnp.sum(u * value, axis=1, keepdims=True))
    za[own_u : own_u + rows] = dz.astype(BF16)
    a_start(2, za)

    arrived(qrecv.at[0], qs_sem.at[0], qr_sem.at[0], partner)
    arrived(qrecv.at[1], qs_sem.at[1], qr_sem.at[1], partner)
    base = 2 * quarter

    def mine(dp):
        r = slice(dp * rows, (dp + 1) * rows)
        return dtx[base + dp * rows : base + (dp + 1) * rows] + qrecv[0, r].astype(F32) + qrecv[1, r].astype(F32)

    for dp in (2, 1, 3):
        i = dp - 1
        tsend[i] = mine(dp).astype(BF16)
        send(tsend.at[i], trecv.at[i], ts_sem.at[i], tr_sem.at[i], dev_b(dp, 0))
    a_step(2, za, 1)
    a_step(2, za, 2)
    caption = mine(0)
    for i in range(3):
        arrived(trecv.at[i], ts_sem.at[i], tr_sem.at[i], partner)
        caption = caption + trecv[i].astype(F32)
    dtext_out[...] = caption
    a_step(2, za, 3)
    a_step(2, za, 4)
    a_finish(2, za)

    for yl in range(2):
        c0 = pl.multiple_of(256 * core + 512 * yl, 128)
        out = lax.dot_general(
            fsel[...], za[:, pl.ds(c0, 384)], (((0,), (0,)), ((), ())), preferred_element_type=F32
        )
        out = out.reshape(8, 32, 384)
        pf[yl] = out
        pb[yl] = out.astype(BF16)
    for dx, dy in [(2, 2), (2, 1), (2, 3), (1, 2), (3, 2), (1, 1), (3, 1), (1, 3), (3, 3),
                   (2, 0), (0, 2), (1, 0), (3, 0), (0, 1), (0, 3)]:
        tx, ty = (x + dx) % NX, (y + dy) % NY
        i = ((4 - dy) % 4) * 4 + (4 - dx) % 4
        send(
            pb.at[ty % 2, (ty // 2) * 4 + tx], precvb.at[i], fs_sem.at[i], fr_sem.at[i], dev(dx=dx, dy=dy)
        )
    acc = pf[y % 2, (y // 2) * 4 + x]
    for i in range(1, 16):
        arrived(precvb.at[i], fs_sem.at[i], fr_sem.at[i], partner)
        acc = acc + precvb[i].astype(F32)
    fin[...] = acc
    for n in range(4):
        @pl.when(narrow == n)
        def _():
            dproj_out[...] = fin[:18, 32 * n : 32 * n + 288]

    for copy in sends:
        copy.wait_send()


def local(image_feats, proj_weight, text_embed, log_scale, logit_bias):
    rows, width = image_feats.shape
    vmem = pl.BlockSpec(memory_space=pltpu.VMEM)
    smem = pl.BlockSpec(memory_space=pltpu.SMEM)
    group = 16 * rows
    dma = pltpu.SemaphoreType.DMA
    loss, d_text, d_proj = pl.pallas_call(
        kernel,
        out_shape=(
            jax.ShapeDtypeStruct((rows, 128), F32),
            jax.ShapeDtypeStruct((rows, width), F32),
            jax.ShapeDtypeStruct((width // 64, width // 4), F32),
        ),
        in_specs=[smem, smem, vmem, pl.BlockSpec(memory_space=pl.ANY), vmem],
        out_specs=(vmem, vmem, vmem),
        scratch_shapes=[
            pltpu.VMEM((width, width), BF16),
            pltpu.VMEM((group, width), BF16),
            pltpu.VMEM((group, width), BF16),
            pltpu.VMEM((group, width), BF16),
            pltpu.VMEM((group, width), BF16),
            pltpu.VMEM((2, group, group // 2), BF16),
            pltpu.VMEM((rows, width), F32),
            pltpu.VMEM((rows, 128), F32),
            pltpu.VMEM((group, width), F32),
            pltpu.VMEM((group, 128), F32),
            pltpu.VMEM((8, rows, width + 128), BF16),
            pltpu.VMEM((8, rows, width + 128), BF16),
            pltpu.VMEM((7, rows, width + 128), BF16),
            pltpu.VMEM((7, rows, width + 128), BF16),
            pltpu.VMEM((group, width), F32),
            pltpu.VMEM((4 * rows, width), BF16),
            pltpu.VMEM((2, 2 * rows, width), BF16),
            pltpu.VMEM((2, 4 * rows, width), BF16),
            pltpu.VMEM((2, 4 * rows, width), BF16),
            pltpu.VMEM((3, rows, width), BF16),
            pltpu.VMEM((3, rows, width), BF16),
            pltpu.VMEM((group, 256), BF16),
            pltpu.VMEM((2, 8, 32, 384), F32),
            pltpu.VMEM((2, 8, 32, 384), BF16),
            pltpu.VMEM((16, 32, 384), BF16),
            pltpu.VMEM((32, 384), F32),
            dma,
            dma((3, 8, 3)), dma((3, 8, 3)), dma((3, 8, 3)), dma((3, 8, 3)),
            dma((16,)), dma((16,)),
            dma((8,)), dma((8,)), dma((7,)), dma((7,)),
            dma((2,)), dma((2,)), dma((2,)), dma((2,)), dma((3,)), dma((3,)),
            dma((16,)), dma((16,)),
        ],
        compiler_params=pltpu.CompilerParams(
            collective_id=0, has_side_effects=True, vmem_limit_bytes=60 * 1024 * 1024
        ),
    )(log_scale, logit_bias, image_feats, proj_weight, text_embed)
    return loss[:, 0], d_text, d_proj


def solution(mesh):
    placed = (P(("wide", "narrow"), None), P(), P(("wide", "narrow"), None), P(), P())
    return jax.shard_map(
        local,
        mesh=mesh,
        in_specs=placed,
        out_specs=(P(("wide", "narrow")), P(("wide", "narrow"), None), P("wide", "narrow")),
        check_vma=False,
    )
```

time: 1900 us -> 94.8 us (0.05)
  waiting for transfers between devices: 1350 us -> 0 us
  matrix products: 359 us -> 0 us
  local copies, waits for them, and re-layouts: 105 us -> 4.38 us
  Pallas kernels: 0 us -> 88.1 us
  blocking collectives: 58 us -> 0 us
    unnamed x4 -> x0, waiting for transfers between devices: 660 us -> none
    ppermute x127 -> x0, waiting for transfers between devices: 659 us -> none  [passed_along(): return lax.ppermute(value, axis, pairs)]
    dot_general x194 -> x0, matrix products: 359 us -> none  [the longest x65 133 us: transposed_product(): lax.dot_general(grad_tile, group_img, (((0,), (0,)), ((), ())), preferred...]
    while x63 -> x0, local copies, waits for them, and re-layouts: 96.9 us -> none
    pallas_call x0 -> x1, Pallas kernels: none -> 88.1 us  [local(): pl.pallas_call(kernel, out_shape=(jax.ShapeDtypeStruct((rows, 128), F32),...]
    unnamed x1 -> x0, blocking collectives: 48.2 us -> none
    reduce_scatter x2 -> x0, waiting for transfers between devices: 29.7 us -> none  [the longest x1 18.5 us: local(): lax.psum_scatter(d_img, 'narrow', scatter_dimension=0, tiled=True)]
  transfers between devices with their start and end apart: 130 -> 0, of which waited for: 129 -> 0; matrix products, arithmetic and copies ran while one was open for 19% -> 0% of each run, Pallas kernels for 0% -> 0%
where the time goes in v1:
time: 94.8 us; the launch traced here: 94.5 us
  Pallas kernels  88.1 us (93%)
  local copies, waits for them, and re-layouts  4.38 us (5%)
  between operations  1.93 us (2%)
    pallas_call x1, Pallas kernels, local(): pl.pallas_call(kernel, out_shape=(jax.ShapeDtypeStruct((rows, 128), F32),...  88.1 us
    unnamed x2, local copies, waits for them, and re-layouts  3.02 us

profile of v1, /device:TPU:1, one launch (start us, length us, event | category | flops | bytes accessed | tf_op | source)
XLA Modules:
  0.0 94.5 jit_solution(5753651818033445204)
XLA Ops:
  1.9 88.1 %shard_map.76 = (f32[48,128]{1,0:T(8,128)}, f32[48,1152]{1,0:T(8,128)}, f32[18,288]{1,0:T(8,128)}) custom-call(f32[1]{0:T(128)S(6)} %copy.10.scale_ref, f32[1]{0:T(128)S(6)} %copy.11.shift_ref, bf16[48,1152]{1,0:T(8,128)(2,1)} %feats_ref.1, bf16[1152,1152]{1,0:T(8,128)(2,1)} %w_hbm.1, bf16[48,1152]{1,0:T(8,128)(2,1)} %text_ref.1), custom_call_target="tpu_custom_call" | custom-call | tf_op jit(solution)/shard_map/pallas_call | solution.py:393
  90.1 1.4 %slice_reduce_fusion = f32[48]{0:T(128)} fusion(f32[48,128]{1,0:T(8,128)} %get-tuple-element.6), kind=kLoop, calls=%fused_computation | loop fusion | bytes 384 | tf_op jit(solution)/shard_map/slice | solution.py:440
  91.4 1.6 %copy.12 = f32[48,1152]{1,0:T(8,128)} copy(f32[48,1152]{1,0:T(8,128)} %get-tuple-element.13) | data formatting | bytes 442368
  93.1 1.4 %copy.13 = f32[18,288]{1,0:T(8,128)} copy(f32[18,288]{1,0:T(8,128)} %get-tuple-element.14) | data formatting | bytes 41472

commit v2 on v1

v2 whole, which is shorter than its diff:
```python
import functools

import jax
import jax.numpy as jnp
from jax import lax
from jax.experimental import pallas as pl
from jax.experimental.pallas import tpu as pltpu
from jax.sharding import PartitionSpec as P

MESH = pl.DeviceIdType.MESH
F32 = jnp.float32
BF16 = jnp.bfloat16

NX, NY, NZ = 4, 4, 8
STREAM = ("L4", "L3", "S3", "L2", "S2", "L1", "S1", "0")
SLOTS = (
    ("X", "L4"), ("X", "L3"), ("X", "S3"), ("O", "L4"), ("O", "L3"), ("O", "S3"),
    ("X", "L2"), ("X", "S2"), ("O", "L2"), ("O", "S2"),
    ("X", "L1"), ("X", "S1"), ("X", "0"), ("O", "L1"), ("O", "S1"), ("O", "0"),
)
SLOT_ROW = {name: i for i, name in enumerate(SLOTS)}
BATCHES = ((0, 6), (6, 10), (10, 16))
RING = STREAM[:7]
ROW_OF_DQ = {2: 0, 1: 1, 0: 2, 3: 3}


def kernel(
    scale_hbm, shift_hbm, feats_hbm, w_hbm, text_hbm,
    loss_hbm, dtext_hbm, dproj_hbm,
    scale_ref, shift_ref, feats_ref, text_ref, wv, ua, za, ta, g, unit, inv, dimg, lossp, psend, precv, rsend, rrecv,
    dtx, hsend, hrecv, qsend, qrecv, tsend, trecv, fsel, fsend, pf, pb, precvb, fin, loss_out, dtext_out, dproj_out,
    in_sem, out_sem, a_send, a_ring_recv, a_part_recv,
    b_send, b_recv, f_send, f_recv, ps_sem, pr_sem, rs_sem, rr_sem,
    hs_sem, hr_sem, qs_sem, qr_sem, ts_sem, tr_sem, fs_sem, fr_sem,
):
    rows, width = feats_ref.shape
    inputs = [
        pltpu.make_async_copy(src, dst, in_sem.at[i])
        for i, (src, dst) in enumerate((
            (text_hbm, text_ref), (feats_hbm, feats_ref), (w_hbm, wv), (scale_hbm, scale_ref), (shift_hbm, shift_ref),
        ))
    ]
    for copy in inputs:
        copy.start()
    chunk = 16
    n_chunk = rows // chunk
    wide = lax.axis_index("wide")
    narrow = lax.axis_index("narrow")
    x = wide % NX
    z = (wide // NX) % NZ
    y = (wide // (NX * NZ)) * 2 + narrow // 2
    core = narrow % 2

    def dev(dx=0, dy=0, dz=0, other=False):
        tx = (x + dx) % NX
        ty = (y + dy) % NY
        tz = (z + dz) % NZ
        tc = (1 - core) if other else core
        return ((ty // 2) * (NX * NZ) + tz * NX + tx, (ty % 2) * 2 + tc)

    def dev_b(dp, dq):
        return dev(dx=dp * (1 - core) + dq * core, dy=dp * core + dq * (1 - core))

    step_z = 1 + core * (NZ - 2)
    along = dev(dz=step_z)
    against = dev(dz=NZ - step_z)
    partner = dev(other=True)

    def rcopy(src, dst, ssem, rsem, target):
        return pltpu.make_async_remote_copy(
            src_ref=src, dst_ref=dst, send_sem=ssem, recv_sem=rsem,
            device_id=target, device_id_type=MESH,
        )

    sends = []

    def send(src, dst, ssem, rsem, target, keep=True):
        copy = rcopy(src, dst, ssem, rsem, target)
        copy.start()
        if keep:
            sends.append(copy)

    def sent(buf, ssem, blocks):
        part_of = buf.at[pl.ds(0, blocks * rows)]
        rcopy(part_of, part_of, ssem, ssem, partner).wait_send()

    def arrived(dst, ssem, rsem, target):
        rcopy(dst, dst, ssem, rsem, target).wait_recv()

    barrier = pltpu.get_barrier_semaphore()
    peers = [dev_b(dp, dq) for dp in range(4) for dq in range(4) if (dp, dq) != (0, 0)]
    hops = [(m, other) for m in range(8) for other in (False, True) if (m, other) != (0, False)]
    peers += [dev(dz=m * step_z, other=other) for m, other in hops]
    for peer in peers:
        pl.semaphore_signal(barrier, inc=1, device_id=peer, device_id_type=MESH)

    def part(buf, slot, c):
        return buf.at[pl.ds(SLOT_ROW[slot] * rows + c * chunk, chunk)]

    def a_copy(k, buf, name, c, to_name, target):
        i = STREAM.index(to_name)
        send(
            part(buf, ("O", name), c), part(buf, ("O", to_name), c),
            a_send.at[k], a_ring_recv.at[k, i, c], target, keep=False,
        )

    def a_hand(k, buf, name, c):
        i = STREAM.index(name)
        send(
            part(buf, ("O", name), c), part(buf, ("X", name), c),
            a_send.at[k], a_part_recv.at[k, i, c], partner, keep=False,
        )

    def a_start(k, buf):
        for c in range(n_chunk):
            a_copy(k, buf, "0", c, "L1", along)
            a_copy(k, buf, "0", c, "S1", against)
            a_hand(k, buf, "0", c)

    def a_wait(k, buf, name, c):
        i = STREAM.index(name)
        arrived(part(buf, ("O", name), c), a_send.at[k], a_ring_recv.at[k, i, c], along)

    def a_step(k, buf, n):
        for c in range(n_chunk):
            a_wait(k, buf, f"L{n}", c)
            if n < 4:
                a_copy(k, buf, f"L{n}", c, f"L{n + 1}", along)
            a_hand(k, buf, f"L{n}", c)
            if n <= 3:
                a_wait(k, buf, f"S{n}", c)
                if n < 3:
                    a_copy(k, buf, f"S{n}", c, f"S{n + 1}", against)
                a_hand(k, buf, f"S{n}", c)

    def a_finish(k, buf, names=STREAM):
        for name in names:
            i = STREAM.index(name)
            for c in range(n_chunk):
                arrived(part(buf, ("X", name), c), a_send.at[k], a_part_recv.at[k, i, c], partner)

    def t_part(dp, dq, c):
        return ta.at[pl.ds((ROW_OF_DQ[dq % 4] * 4 + dp % 4) * rows + c * chunk, chunk)]

    def b_copy(dp, dq, mp, mq, c):
        to = ((dp - mp) % 4, (dq - mq) % 4)
        send(
            t_part(dp, dq, c), t_part(*to, c), b_send, b_recv.at[to[1] * 4 + to[0], c],
            dev_b(mp % 4, mq % 4), keep=False,
        )

    def b_wait(dp, dq, c):
        part_of = t_part(dp, dq, c)
        arrived(part_of, b_send, b_recv.at[dq * 4 + dp, c], partner)

    def b_spread(dp, c):
        b_copy(dp, 0, 0, 1, c)
        b_copy(dp, 0, 0, -1, c)

    def each_chunk(step):
        for c in range(n_chunk):
            step(c)

    def b_start(c):
        b_copy(0, 0, 1, 0, c)
        b_copy(0, 0, -1, 0, c)
        b_spread(0, c)

    def b_first(c):
        b_wait(3, 0, c)
        b_copy(3, 0, 1, 0, c)
        b_spread(3, c)
        b_wait(1, 0, c)
        b_spread(1, c)
        b_wait(0, 1, c)
        b_copy(0, 1, 0, -1, c)

    def b_second(c):
        b_wait(2, 0, c)
        b_spread(2, c)
        b_wait(3, 3, c)
        b_copy(3, 3, 0, 1, c)
        b_wait(1, 1, c)
        b_copy(1, 1, 0, -1, c)

    def b_third(c):
        b_wait(2, 3, c)
        b_copy(2, 3, 0, 1, c)
        b_wait(0, 3, c)
        b_wait(1, 3, c)

    def b_last(c):
        for dp, dq in ((3, 1), (2, 1), (0, 2), (3, 2), (1, 2), (2, 2)):
            b_wait(dp, dq, c)

    inputs[0].wait()
    text = text_ref[...].astype(F32)
    text_inv = lax.rsqrt(jnp.sum(text * text, axis=1, keepdims=True) + 1e-06)
    own_t = ROW_OF_DQ[0] * 4 * rows
    ta[own_t : own_t + rows] = (text * text_inv).astype(BF16)
    own_u = SLOT_ROW[("O", "0")] * rows
    inputs[1].wait()

    pl.semaphore_wait(barrier, len(peers))
    each_chunk(b_start)

    for copy in inputs[2:]:
        copy.wait()
    zproj = jnp.dot(feats_ref[...], wv[...], preferred_element_type=F32)
    img_inv = lax.rsqrt(jnp.sum(zproj * zproj, axis=1, keepdims=True) + 1e-06)
    img_unit = zproj * img_inv
    unit[...] = img_unit
    inv[...] = jnp.broadcast_to(img_inv, inv.shape)
    ua[own_u : own_u + rows] = img_unit.astype(BF16)
    a_start(0, ua)

    pick_row = lax.broadcasted_iota(jnp.int32, (width, 256), 0)
    pick_col = lax.broadcasted_iota(jnp.int32, (width, 256), 1)
    combo = pick_col >> 5
    inner = pick_col & 31
    first = jnp.where(inner < 18, 18 * (32 * (combo >> 2) + (combo & 3)) + inner - pick_row, 4 * width)

    def pick(m):
        tz = (z + m * step_z) % NZ
        chosen = jnp.where(first + 72 * tz == 0, 1.0, 0.0).astype(BF16)
        fsend[m] = jnp.dot(feats_ref[...], chosen, preferred_element_type=F32).astype(BF16)

    def pick_sends():
        r = pl.ds(SLOT_ROW[("O", "0")] * rows, rows)
        fsel[r] = fsend[0]
        for m, other in hops:
            i = SLOT_ROW[("X" if other else "O", f"L{m}" if 1 <= m <= 4 else f"S{8 - m}" if m else "0")]
            send(
                fsend.at[m], fsel.at[pl.ds(i * rows, rows)], f_send, f_recv.at[i],
                dev(dz=m * step_z, other=other), keep=False,
            )

    def pick_wait():
        for i in range(16):
            if i != SLOT_ROW[("O", "0")]:
                arrived(fsel.at[pl.ds(i * rows, rows)], f_send, f_recv.at[i], partner)

    scale = jnp.exp(jnp.full((1, 128), scale_ref[0], F32))[:, :1]
    shift = shift_ref[0]
    half = 8 * rows

    def cell(batch, pair):
        r0, r1 = (rows * b for b in BATCHES[batch])
        prod = lax.dot_general(
            ua[r0:r1, :], ta[pair * half : (pair + 1) * half, :], (((1,), (1,)), ((), ())),
            preferred_element_type=F32,
        )
        total = None
        for j in range(half // 128):
            logit = scale * prod[:, 128 * j : 128 * (j + 1)] + shift
            factor = scale
            if j == 0 and pair == 1 and r1 > own_u:
                row = lax.broadcasted_iota(jnp.int32, logit.shape, 0) + (r0 - own_u)
                own = row == lax.broadcasted_iota(jnp.int32, logit.shape, 1)
                logit = jnp.where(own, -logit, logit)
                factor = jnp.where(own, -scale, scale)
            e = jnp.exp(logit)
            g[pair, r0:r1, 128 * j : 128 * (j + 1)] = (factor * (e / (1.0 + e))).astype(BF16)
            term = jnp.log1p(e)
            total = term if total is None else total + term
        if pair == 1:
            lossp[r0:r1, :] = total
        else:
            lossp[r0:r1, :] += total

    pick(0)
    pick(1)
    each_chunk(b_first)
    a_step(0, ua, 1)
    pick(2)
    pick(3)
    a_step(0, ua, 2)
    each_chunk(b_second)
    pick(4)
    pick(5)
    a_step(0, ua, 3)
    pick(6)
    pick(7)
    each_chunk(b_third)
    a_finish(0, ua, ("0", "L1", "S1"))
    cell(2, 1)
    a_step(0, ua, 4)
    pick_sends()
    a_finish(0, ua, ("L2", "S2"))
    cell(1, 1)
    each_chunk(b_last)
    cell(2, 0)
    cell(1, 0)
    a_finish(0, ua, ("L3", "S3", "L4"))
    cell(0, 1)
    cell(0, 0)

    def slot_rows(slot, c=None):
        if c is None:
            return pl.ds(SLOT_ROW[slot] * rows, rows)
        return pl.ds(SLOT_ROW[slot] * rows + c * chunk, chunk)

    def pack(ref, i, r, value, loss):
        lane = lax.broadcasted_iota(jnp.int32, (value.shape[0], 128), 1)
        hi = loss.astype(BF16).astype(F32)
        lo = loss - hi
        ref[i, r, :width] = value.astype(BF16)
        ref[i, r, width:] = jnp.where(lane == 0, hi, jnp.where(lane == 1, lo, 0.0)).astype(BF16)

    def unpack(ref, i, r):
        tail = ref[i, r, width:].astype(F32)
        return ref[i, r, :width].astype(F32), jnp.sum(tail, axis=1, keepdims=True)

    def own_part(slot, c=None):
        r = slot_rows(slot, c)
        return dimg[r, :], jnp.sum(lossp[r, :], axis=1, keepdims=True)

    def image_batch(b):
        lo, hi = BATCHES[b]
        r = slice(lo * rows, hi * rows)
        acc = jnp.dot(g[0, r, :], ta[:half], preferred_element_type=F32)
        acc += jnp.dot(g[1, r, :], ta[half:], preferred_element_type=F32)
        dimg[r, :] = acc
        for kind, name in SLOTS[lo:hi]:
            if kind == "X":
                i = STREAM.index(name)
                pack(psend, i, slice(0, rows), *own_part((kind, name)))
                send(psend.at[i], precv.at[i], ps_sem.at[i], pr_sem.at[i], partner)

    def handed(name):
        i = STREAM.index(name)
        arrived(precv.at[i], ps_sem.at[i], pr_sem.at[i], partner)

    def gathered(name, c):
        r = slice(c * chunk, (c + 1) * chunk)
        value, loss = own_part(("O", name), c)
        more, more_loss = unpack(precv, STREAM.index(name), r)
        value, loss = value + more, loss + more_loss
        if name == "0":
            before = ["L1", "S1"]
        elif name in ("L4", "S3"):
            before = []
        else:
            before = [name[0] + str(int(name[1]) + 1)]
        for prev in before:
            j = RING.index(prev)
            arrived(rrecv.at[j, r], rs_sem.at[j], rr_sem.at[j, c], along)
            more, more_loss = unpack(rrecv, j, r)
            value, loss = value + more, loss + more_loss
        return value, loss

    def ring(*names):
        for name in names:
            handed(name)
        for c in range(n_chunk):
            r = slice(c * chunk, (c + 1) * chunk)
            for name in names:
                i = RING.index(name)
                pack(rsend, i, r, *gathered(name, c))
                send(
                    rsend.at[i, r], rrecv.at[i, r], rs_sem.at[i], rr_sem.at[i, c],
                    against if name[0] == "L" else along, keep=False,
                )

    def caption_half(k):
        dtx[k * half : (k + 1) * half, :] = lax.dot_general(
            g[k], ua[...], (((0,), (0,)), ((), ())), preferred_element_type=F32
        )

    quarter = 4 * rows
    image_batch(0)
    image_batch(1)
    ring("L4")
    image_batch(2)
    ring("L3", "S3")
    caption_half(0)
    hsend[...] = dtx[:quarter].astype(BF16)
    send(hsend.at[: quarter // 2], hrecv.at[0], hs_sem.at[0], hr_sem.at[0], dev_b(0, 1))
    send(hsend.at[quarter // 2 :], hrecv.at[1], hs_sem.at[1], hr_sem.at[1], dev_b(0, 3))
    ring("L2", "S2")
    caption_half(1)

    arrived(hrecv.at[0], hs_sem.at[0], hr_sem.at[0], partner)
    h = quarter // 2
    up, down = quarter, 3 * quarter
    qsend[0, :h] = (dtx[up : up + h] + hrecv[0].astype(F32)).astype(BF16)
    qsend[0, h:] = dtx[up + h : up + quarter].astype(BF16)
    send(qsend.at[0], qrecv.at[0], qs_sem.at[0], qr_sem.at[0], dev_b(0, 1))
    arrived(hrecv.at[1], hs_sem.at[1], hr_sem.at[1], partner)
    qsend[1, :h] = dtx[down : down + h].astype(BF16)
    qsend[1, h:] = (dtx[down + h : down + quarter] + hrecv[1].astype(F32)).astype(BF16)
    send(qsend.at[1], qrecv.at[1], qs_sem.at[1], qr_sem.at[1], dev_b(0, 3))

    ring("L1", "S1")
    handed("0")
    for c in range(n_chunk):
        r = slice(c * chunk, (c + 1) * chunk)
        value, loss = gathered("0", c)
        loss_out[r, :] = jnp.broadcast_to(loss, (chunk, 128))
        u = unit[r, :]
        dz = inv[r, :1] * (value - u * jnp.sum(u * value, axis=1, keepdims=True))
        za[own_u + c * chunk : own_u + (c + 1) * chunk] = dz.astype(BF16)
        a_copy(1, za, "0", c, "L1", along)
        a_copy(1, za, "0", c, "S1", against)
        a_hand(1, za, "0", c)

    arrived(qrecv.at[0], qs_sem.at[0], qr_sem.at[0], partner)
    arrived(qrecv.at[1], qs_sem.at[1], qr_sem.at[1], partner)
    base = 2 * quarter

    def mine(dp):
        r = slice(dp * rows, (dp + 1) * rows)
        return dtx[base + dp * rows : base + (dp + 1) * rows] + qrecv[0, r].astype(F32) + qrecv[1, r].astype(F32)

    for dp in (2, 1, 3):
        i = dp - 1
        tsend[i] = mine(dp).astype(BF16)
        send(tsend.at[i], trecv.at[i], ts_sem.at[i], tr_sem.at[i], dev_b(dp, 0))
    a_step(1, za, 1)
    a_step(1, za, 2)
    caption = mine(0)
    for i in range(3):
        arrived(trecv.at[i], ts_sem.at[i], tr_sem.at[i], partner)
        caption = caption + trecv[i].astype(F32)
    dtext_out[...] = caption
    outputs = [
        pltpu.make_async_copy(src, dst, out_sem.at[i])
        for i, (src, dst) in enumerate(((loss_out, loss_hbm), (dtext_out, dtext_hbm), (dproj_out, dproj_hbm)))
    ]
    outputs[0].start()
    outputs[1].start()
    a_step(1, za, 3)
    a_step(1, za, 4)
    a_finish(1, za)

    pick_wait()
    for yl in range(2):
        c0 = pl.multiple_of(256 * core + 512 * yl, 128)
        out = lax.dot_general(
            fsel[...], za[:, pl.ds(c0, 384)], (((0,), (0,)), ((), ())), preferred_element_type=F32
        )
        out = out.reshape(8, 32, 384)
        pf[yl] = out
        pb[yl] = out.astype(BF16)
    for dx, dy in [(2, 2), (2, 1), (2, 3), (1, 2), (3, 2), (1, 1), (3, 1), (1, 3), (3, 3),
                   (2, 0), (0, 2), (1, 0), (3, 0), (0, 1), (0, 3)]:
        tx, ty = (x + dx) % NX, (y + dy) % NY
        i = ((4 - dy) % 4) * 4 + (4 - dx) % 4
        send(
            pb.at[ty % 2, (ty // 2) * 4 + tx], precvb.at[i], fs_sem.at[i], fr_sem.at[i], dev(dx=dx, dy=dy)
        )
    acc = pf[y % 2, (y // 2) * 4 + x]
    for i in range(1, 16):
        arrived(precvb.at[i], fs_sem.at[i], fr_sem.at[i], partner)
        acc = acc + precvb[i].astype(F32)
    fin[...] = acc
    for n in range(4):
        @pl.when(narrow == n)
        def _():
            dproj_out[...] = fin[:18, 32 * n : 32 * n + 288]

    outputs[2].start()
    for copy in sends:
        copy.wait_send()
    for i in range(7):
        rcopy(rsend.at[i], rsend.at[i], rs_sem.at[i], rs_sem.at[i], partner).wait_send()
    for k, buf in enumerate((ua, za)):
        sent(buf, a_send.at[k], 15)
    sent(ta, b_send, 15)
    sent(fsel, f_send, 15)
    for copy in outputs:
        copy.wait()


def results(loss_ref, dtext_ref, dproj_ref, loss_out, dtext_out, dproj_out):
    loss_out[...] = jnp.transpose(loss_ref[...])[:1, :]
    dtext_out[...] = dtext_ref[...]
    dproj_out[...] = dproj_ref[...]


def local(image_feats, proj_weight, text_embed, log_scale, logit_bias):
    rows, width = image_feats.shape
    vmem = pl.BlockSpec(memory_space=pltpu.VMEM)
    anywhere = pl.BlockSpec(memory_space=pl.ANY)
    group = 16 * rows
    dma = pltpu.SemaphoreType.DMA
    loss, d_text, d_proj = pl.pallas_call(
        kernel,
        out_shape=(
            jax.ShapeDtypeStruct((rows, 128), F32),
            jax.ShapeDtypeStruct((rows, width), F32),
            jax.ShapeDtypeStruct((width // 64, width // 4), F32),
        ),
        in_specs=[anywhere] * 5,
        out_specs=(anywhere, anywhere, anywhere),
        scratch_shapes=[
            pltpu.SMEM((1,), F32),
            pltpu.SMEM((1,), F32),
            pltpu.VMEM((rows, width), BF16),
            pltpu.VMEM((rows, width), BF16),
            pltpu.VMEM((width, width), BF16),
            pltpu.VMEM((group, width), BF16),
            pltpu.VMEM((group, width), BF16),
            pltpu.VMEM((group, width), BF16),
            pltpu.VMEM((2, group, group // 2), BF16),
            pltpu.VMEM((rows, width), F32),
            pltpu.VMEM((rows, 128), F32),
            pltpu.VMEM((group, width), F32),
            pltpu.VMEM((group, 128), F32),
            pltpu.VMEM((8, rows, width + 128), BF16),
            pltpu.VMEM((8, rows, width + 128), BF16),
            pltpu.VMEM((7, rows, width + 128), BF16),
            pltpu.VMEM((7, rows, width + 128), BF16),
            pltpu.VMEM((group, width), F32),
            pltpu.VMEM((4 * rows, width), BF16),
            pltpu.VMEM((2, 2 * rows, width), BF16),
            pltpu.VMEM((2, 4 * rows, width), BF16),
            pltpu.VMEM((2, 4 * rows, width), BF16),
            pltpu.VMEM((3, rows, width), BF16),
            pltpu.VMEM((3, rows, width), BF16),
            pltpu.VMEM((group, 256), BF16),
            pltpu.VMEM((8, rows, 256), BF16),
            pltpu.VMEM((2, 8, 32, 384), F32),
            pltpu.VMEM((2, 8, 32, 384), BF16),
            pltpu.VMEM((16, 32, 384), BF16),
            pltpu.VMEM((32, 384), F32),
            pltpu.VMEM((rows, 128), F32),
            pltpu.VMEM((rows, width), F32),
            pltpu.VMEM((width // 64, width // 4), F32),
            dma((5,)), dma((3,)), dma((2,)), dma((2, 8, 3)), dma((2, 8, 3)),
            dma, dma((16, 3)), dma, dma((16,)),
            dma((8,)), dma((8,)), dma((7,)), dma((7, 3)),
            dma((2,)), dma((2,)), dma((2,)), dma((2,)), dma((3,)), dma((3,)),
            dma((16,)), dma((16,)),
        ],
        compiler_params=pltpu.CompilerParams(
            collective_id=0, has_side_effects=True, vmem_limit_bytes=60 * 1024 * 1024
        ),
    )(log_scale, logit_bias, image_feats, proj_weight, text_embed)
    loss, d_text, d_proj = pl.pallas_call(
        results,
        out_shape=(
            jax.ShapeDtypeStruct((1, rows), F32),
            jax.ShapeDtypeStruct(d_text.shape, F32),
            jax.ShapeDtypeStruct(d_proj.shape, F32),
        ),
        in_specs=[vmem, vmem, vmem],
        out_specs=(vmem, vmem, vmem),
    )(loss, d_text, d_proj)
    return loss.reshape(rows), d_text, d_proj


def solution(mesh):
    placed = (P(("wide", "narrow"), None), P(), P(("wide", "narrow"), None), P(), P())
    return jax.shard_map(
        local,
        mesh=mesh,
        in_specs=placed,
        out_specs=(P(("wide", "narrow")), P(("wide", "narrow"), None), P("wide", "narrow")),
        check_vma=False,
    )
```

time: 94.8 us -> 80.7 us (0.85)
  Pallas kernels: 88.1 us -> 78.6 us
  local copies, waits for them, and re-layouts: 4.38 us -> 0 us
    pallas_call x1, Pallas kernels: 88.1 us -> 77 us  [local(): pl.pallas_call(kernel, out_shape=(jax.ShapeDtypeStruct((rows, 128), F32),...]
    unnamed x2 -> x0, local copies, waits for them, and re-layouts: 3.02 us -> none
    pallas_call x0 -> x1, Pallas kernels: none -> 1.64 us  [local(): pl.pallas_call(results, out_shape=(jax.ShapeDtypeStruct((1, rows), F32),...]
    slice x1 -> x0, local copies, waits for them, and re-layouts: 1.36 us -> none  [local(): return (loss[:, 0], d_text, d_proj)]
where the time goes in v2:
time: 80.7 us; the launch traced here: 80.6 us
  Pallas kernels  78.6 us (97%)
  between operations  1.93 us (2%)
    pallas_call x1, Pallas kernels, local(): pl.pallas_call(kernel, out_shape=(jax.ShapeDtypeStruct((rows, 128), F32),...  77 us
    pallas_call x1, Pallas kernels, local(): pl.pallas_call(results, out_shape=(jax.ShapeDtypeStruct((1, rows), F32),...  1.64 us

profile of v2, /device:TPU:1, one launch (start us, length us, event | category | flops | bytes accessed | tf_op | source)
XLA Modules:
  0.0 80.6 jit_solution(17596624312317367639)
XLA Ops:
  1.9 77.0 %shard_map.76 = (f32[48,128]{1,0:T(8,128)}, f32[48,1152]{1,0:T(8,128)}, f32[18,288]{1,0:T(8,128)}) custom-call(f32[1]{0:T(128)S(6)} %copy.8.scale_hbm, f32[1]{0:T(128)S(6)} %copy.9.shift_hbm, bf16[48,1152]{1,0:T(8,128)(2,1)} %feats_hbm.1, bf16[1152,1152]{1,0:T(8,128)(2,1)} %w_hbm.1, bf16[48,1152]{1,0:T(8,128)(2,1)} %text_hbm.1), custom_call_target="tpu_custom_call" | custom-call | tf_op jit(solution)/shard_map/pallas_call | solution.py:487
  78.9 1.6 %shard_map.77 = (f32[1,48]{1,0:T(1,128)}, f32[48,1152]{1,0:T(8,128)}, f32[18,288]{1,0:T(8,128)}) custom-call(f32[48,128]{1,0:T(8,128)} %get-tuple-element.9.loss_ref, f32[48,1152]{1,0:T(8,128)} %get-tuple-element.10.dtext_ref, f32[18,288]{1,0:T(8,128)} %get-tuple-element.11.dproj_ref), custom_call_target="tpu_custom_call" | custom-call | tf_op jit(solution)/shard_map/pallas_call | solution.py:540

commit v3 on v0

v3 whole, which is shorter than its diff:
```python
import functools

import jax
import jax.numpy as jnp
from jax import lax
from jax.experimental import pallas as pl
from jax.experimental.pallas import tpu as pltpu
from jax.sharding import PartitionSpec as P

MESH = pl.DeviceIdType.MESH
F32 = jnp.float32
BF16 = jnp.bfloat16

NX, NY, NZ = 4, 4, 8
STREAM = ("L4", "L3", "S3", "L2", "S2", "L1", "S1", "0")
SLOTS = (
    ("X", "L4"), ("X", "L3"), ("X", "S3"), ("O", "L4"), ("O", "L3"), ("O", "S3"),
    ("X", "L2"), ("X", "S2"), ("O", "L2"), ("O", "S2"),
    ("X", "L1"), ("X", "S1"), ("X", "0"), ("O", "L1"), ("O", "S1"), ("O", "0"),
)
SLOT_ROW = {name: i for i, name in enumerate(SLOTS)}
BATCHES = ((0, 6), (6, 10), (10, 16))
RING = STREAM[:7]
ROW_OF_DQ = {2: 0, 1: 1, 0: 2, 3: 3}


def kernel(
    scale_hbm, shift_hbm, feats_hbm, w_hbm, text_hbm,
    loss_hbm, dtext_hbm, dproj_hbm,
    scale_ref, shift_ref, feats_ref, text_ref, wv, ta, ub, fb, g, loss_acc, loss_send, loss_recv,
    d_text, psend, precv, rsend, rrecv, dzb, qf, qb, pq, qs, qo, qr, ps, pr, fz, zf, zs, zr, fin,
    loss_out, dtext_out, dproj_out,
    in_sem, out_sem, a_send, a_ring_recv, a_part_recv, b_send, b_recv, f_send, f_recv,
    l_send, l_recv, ps_sem, pr_sem, rs_sem, rr_sem, pq_send, pq_recv,
    qs_sem, qr_sem, ts_sem, tr_sem, zs_sem, zr_sem,
):
    rows, width = feats_ref.shape
    inputs = [
        pltpu.make_async_copy(src, dst, in_sem.at[i])
        for i, (src, dst) in enumerate((
            (text_hbm, text_ref), (feats_hbm, feats_ref), (w_hbm, wv), (scale_hbm, scale_ref), (shift_hbm, shift_ref),
        ))
    ]
    for copy in inputs:
        copy.start()
    chunk = 16
    n_chunk = rows // chunk
    wide = lax.axis_index("wide")
    narrow = lax.axis_index("narrow")
    x = wide % NX
    z = (wide // NX) % NZ
    y = (wide // (NX * NZ)) * 2 + narrow // 2
    core = narrow % 2

    def dev(dx=0, dy=0, dz=0, other=False):
        tx = (x + dx) % NX
        ty = (y + dy) % NY
        tz = (z + dz) % NZ
        tc = (1 - core) if other else core
        return ((ty // 2) * (NX * NZ) + tz * NX + tx, (ty % 2) * 2 + tc)

    def dev_b(dp, dq):
        return dev(dx=dp * (1 - core) + dq * core, dy=dp * core + dq * (1 - core))

    step_z = 1 + core * (NZ - 2)
    along = dev(dz=step_z)
    against = dev(dz=NZ - step_z)
    partner = dev(other=True)

    def rcopy(src, dst, ssem, rsem, target):
        return pltpu.make_async_remote_copy(
            src_ref=src, dst_ref=dst, send_sem=ssem, recv_sem=rsem,
            device_id=target, device_id_type=MESH,
        )

    sends = []

    def send(src, dst, ssem, rsem, target, keep=True):
        copy = rcopy(src, dst, ssem, rsem, target)
        copy.start()
        if keep:
            sends.append(copy)

    def sent(part_of, ssem):
        rcopy(part_of, part_of, ssem, ssem, partner).wait_send()

    def arrived(dst, rsem):
        rcopy(dst, dst, rsem, rsem, partner).wait_recv()

    barrier = pltpu.get_barrier_semaphore()
    peers = [dev_b(dp, dq) for dp in range(4) for dq in range(4) if (dp, dq) != (0, 0)]
    peers += [dev(dz=dz) for dz in range(1, 8)] + [partner]
    for peer in peers:
        pl.semaphore_signal(barrier, inc=1, device_id=peer, device_id_type=MESH)

    def a_part(slot, c):
        return ta.at[pl.ds(SLOT_ROW[slot] * rows + c * chunk, chunk)]

    def a_copy(name, c, to_name, target):
        i = STREAM.index(to_name)
        send(a_part(("O", name), c), a_part(("O", to_name), c), a_send, a_ring_recv.at[i, c], target, keep=False)

    def a_hand(name, c):
        i = STREAM.index(name)
        send(a_part(("O", name), c), a_part(("X", name), c), a_send, a_part_recv.at[i, c], partner, keep=False)

    def a_start():
        for c in range(n_chunk):
            a_copy("0", c, "L1", along)
            a_copy("0", c, "S1", against)
            a_hand("0", c)

    def a_wait(name, c):
        arrived(a_part(("O", name), c), a_ring_recv.at[STREAM.index(name), c])

    def a_step(n):
        for c in range(n_chunk):
            a_wait(f"L{n}", c)
            if n < 4:
                a_copy(f"L{n}", c, f"L{n + 1}", along)
            a_hand(f"L{n}", c)
            if n <= 3:
                a_wait(f"S{n}", c)
                if n < 3:
                    a_copy(f"S{n}", c, f"S{n + 1}", against)
                a_hand(f"S{n}", c)

    def a_finish(*names):
        for name in names:
            for c in range(n_chunk):
                arrived(a_part(("X", name), c), a_part_recv.at[STREAM.index(name), c])

    class Plane:
        def __init__(self, buf, ssem, rsem, size):
            self.buf, self.ssem, self.rsem, self.size = buf, ssem, rsem, size

        def part(self, dp, dq, c):
            return self.buf.at[pl.ds((ROW_OF_DQ[dq % 4] * 4 + dp % 4) * rows + c * self.size, self.size)]

        def copy(self, dp, dq, mp, mq, c):
            to = ((dp - mp) % 4, (dq - mq) % 4)
            send(
                self.part(dp, dq, c), self.part(*to, c), self.ssem, self.rsem.at[to[1] * 4 + to[0], c],
                dev_b(mp % 4, mq % 4), keep=False,
            )

        def wait(self, dp, dq, c):
            arrived(self.part(dp, dq, c), self.rsem.at[dq * 4 + dp, c])

        def spread(self, dp, c):
            self.copy(dp, 0, 0, 1, c)
            self.copy(dp, 0, 0, -1, c)

        def start(self, c):
            self.copy(0, 0, 1, 0, c)
            self.copy(0, 0, -1, 0, c)
            self.spread(0, c)

        def first(self, c):
            self.wait(3, 0, c)
            self.copy(3, 0, 1, 0, c)
            self.spread(3, c)
            self.wait(1, 0, c)
            self.spread(1, c)
            self.wait(0, 1, c)
            self.copy(0, 1, 0, -1, c)

        def second(self, c):
            self.wait(2, 0, c)
            self.spread(2, c)
            self.wait(3, 3, c)
            self.copy(3, 3, 0, 1, c)
            self.wait(1, 1, c)
            self.copy(1, 1, 0, -1, c)

        def third(self, c):
            self.wait(2, 3, c)
            self.copy(2, 3, 0, 1, c)
            self.wait(0, 3, c)
            self.wait(1, 3, c)

        def last(self, c):
            for dp, dq in ((3, 1), (2, 1), (0, 2), (3, 2), (1, 2), (2, 2)):
                self.wait(dp, dq, c)

        def run(self, step):
            for c in range(rows // self.size):
                step(c)

    images = Plane(ub, b_send, b_recv, chunk)
    feats = Plane(fb, f_send, f_recv, rows)

    inputs[0].wait()
    text = text_ref[...].astype(F32)
    text_inv = lax.rsqrt(jnp.sum(text * text, axis=1, keepdims=True) + 1e-06)
    own_a = SLOT_ROW[("O", "0")] * rows
    own_b = ROW_OF_DQ[0] * 4 * rows
    ta[own_a : own_a + rows] = (text * text_inv).astype(BF16)
    inputs[1].wait()
    zs[...] = jnp.zeros_like(zs)
    loss_send[...] = jnp.zeros_like(loss_send)

    pl.semaphore_wait(barrier, len(peers))
    a_start()

    for copy in inputs[2:]:
        copy.wait()
    zproj = jnp.dot(feats_ref[...], wv[...], preferred_element_type=F32)
    img_inv = lax.rsqrt(jnp.sum(zproj * zproj, axis=1, keepdims=True) + 1e-06)
    ub[own_b : own_b + rows] = (zproj * img_inv).astype(BF16)
    images.run(images.start)

    col = lax.broadcasted_iota(jnp.int32, (8, width), 1)
    combo = (col * 911) >> 17
    rest = col - 144 * combo
    layer = (rest * 3641) >> 16
    source = 18 * (32 * (combo >> 2) + 4 * layer + (combo & 3)) + rest - 18 * layer
    order = jnp.where(lax.broadcasted_iota(jnp.int32, (width, width), 0) == source[:1], 1.0, 0.0).astype(BF16)
    fb[own_b : own_b + rows, :width] = jnp.dot(feats_ref[...], order, preferred_element_type=F32).astype(BF16)
    lane = lax.broadcasted_iota(jnp.int32, (rows, 128), 1)
    inv_hi = img_inv.astype(BF16).astype(F32)
    fb[own_b : own_b + rows, width:] = jnp.where(
        lane == 0, inv_hi, jnp.where(lane == 1, img_inv - inv_hi, 0.0)
    ).astype(BF16)

    scale = jnp.exp(jnp.full((1, 128), scale_ref[0], F32))[:, :1]
    shift = shift_ref[0]
    half = 8 * rows

    def cell(batch, pair):
        r0, r1 = (rows * b for b in BATCHES[batch])
        prod = lax.dot_general(
            ta[r0:r1, :], ub[pair * half : (pair + 1) * half, :], (((1,), (1,)), ((), ())),
            preferred_element_type=F32,
        )
        for j in range(half // 128):
            lanes = slice(128 * j, 128 * (j + 1))
            logit = scale * prod[:, lanes] + shift
            factor = scale
            if j == 0 and pair == 1 and r1 > own_a:
                row = lax.broadcasted_iota(jnp.int32, logit.shape, 0) + (r0 - own_a)
                own = row == lax.broadcasted_iota(jnp.int32, logit.shape, 1)
                logit = jnp.where(own, -logit, logit)
                factor = jnp.where(own, -scale, scale)
            e = jnp.exp(logit)
            g[pair, r0:r1, lanes] = (factor * (e / (1.0 + e))).astype(BF16)
            total = jnp.sum(jnp.log1p(e).reshape((r1 - r0) // 8, 8, 128), axis=0)
            if batch == 2:
                loss_acc[pair, :, lanes] = total
            else:
                loss_acc[pair, :, lanes] += total

    a_step(1)
    images.run(images.first)
    a_step(2)
    images.run(images.second)
    a_step(3)
    images.run(images.third)
    a_finish("0", "L1", "S1")
    cell(2, 1)
    a_step(4)
    feats.run(feats.start)
    a_finish("L2", "S2")
    cell(1, 1)
    images.run(images.last)
    cell(2, 0)
    cell(1, 0)
    feats.run(feats.first)
    a_finish("L3", "S3", "L4")
    cell(0, 1)
    cell(0, 0)

    def image_half(pair):
        r = slice(pair * half, (pair + 1) * half)
        d = lax.dot_general(g[pair], ta[...], (((0,), (0,)), ((), ())), preferred_element_type=F32)
        u = ub[r, :].astype(F32)
        factor = jnp.sum(fb[r, width:].astype(F32), axis=1, keepdims=True)
        dzb[r, :] = (factor * (d - u * jnp.sum(u * d, axis=1, keepdims=True))).astype(BF16)

    for pair in range(2):
        summed = jnp.sum(loss_acc[pair], axis=0, keepdims=True)
        for k in range(8):
            loss_send[8 * pair + k, :1, :rows] = summed[:, k * rows : (k + 1) * rows]
    for dq in range(4):
        for dp in range(4):
            if (dp, dq) != (0, 0):
                i = ((4 - dq) % 4) * 4 + (4 - dp) % 4
                k = ROW_OF_DQ[dq] * 4 + dp
                send(loss_send.at[k], loss_recv.at[i], l_send, l_recv.at[i], dev_b(dp, dq), keep=False)

    feats.run(feats.second)
    feats.run(feats.third)
    feats.run(feats.last)
    image_half(1)
    image_half(0)

    block = 384
    for b in range(width // block):
        r = slice(b * block, (b + 1) * block)
        out = lax.dot_general(fb[:, r], dzb[...], (((0,), (0,)), ((), ())), preferred_element_type=F32)
        qf[r, :] = out
        qb[r, :] = out.astype(BF16)
        for yl in range(2):
            lanes = pl.ds(pl.multiple_of(256 * (1 - core) + 512 * yl, 128), 384)
            send(qb.at[r, lanes], pq.at[yl, r], pq_send.at[b, yl], pq_recv.at[b, yl], partner)

    def slot_rows(slot, c=None):
        if c is None:
            return pl.ds(SLOT_ROW[slot] * rows, rows)
        return pl.ds(SLOT_ROW[slot] * rows + c * chunk, chunk)

    def text_batch(b):
        lo, hi = BATCHES[b]
        r = slice(lo * rows, hi * rows)
        acc = jnp.dot(g[0, r, :], ub[:half], preferred_element_type=F32)
        acc += jnp.dot(g[1, r, :], ub[half:], preferred_element_type=F32)
        d_text[r, :] = acc
        for kind, name in SLOTS[lo:hi]:
            if kind == "X":
                i = STREAM.index(name)
                psend[i] = d_text[slot_rows((kind, name)), :].astype(BF16)
                send(psend.at[i], precv.at[i], ps_sem.at[i], pr_sem.at[i], partner)

    def handed(name):
        i = STREAM.index(name)
        arrived(precv.at[i], pr_sem.at[i])

    def gathered(name, c):
        r = slice(c * chunk, (c + 1) * chunk)
        value = d_text[slot_rows(("O", name), c), :] + precv[STREAM.index(name), r].astype(F32)
        if name == "0":
            before = ["L1", "S1"]
        elif name in ("L4", "S3"):
            before = []
        else:
            before = [name[0] + str(int(name[1]) + 1)]
        for prev in before:
            j = RING.index(prev)
            arrived(rrecv.at[j, r], rr_sem.at[j, c])
            value = value + rrecv[j, r].astype(F32)
        return value

    def ring(*names):
        for name in names:
            handed(name)
        for c in range(n_chunk):
            r = slice(c * chunk, (c + 1) * chunk)
            for name in names:
                i = RING.index(name)
                rsend[i, r] = gathered(name, c).astype(BF16)
                send(
                    rsend.at[i, r], rrecv.at[i, r], rs_sem.at[i], rr_sem.at[i, c],
                    against if name[0] == "L" else along, keep=False,
                )

    def unit(dp, dq):
        px = (x + dp * (1 - core) + dq * core) % NX
        py = (y + dp * core + dq * (1 - core)) % NY
        r = pl.ds(pl.multiple_of(144 * ((py // 2) * NX + px), 16), 144)
        lanes = pl.ds(pl.multiple_of(256 * core + 512 * (py % 2), 128), 384)
        return qf[r, lanes] + pq[py % 2, r, :].astype(F32)

    text_batch(0)
    for b in range(width // block):
        for yl in range(2):
            arrived(pq.at[yl, pl.ds(b * block, block)], pq_recv.at[b, yl])
    for dq in (2, 1, 3):
        for dp in range(4):
            qs[dq - 1, dp] = unit(dp, dq).astype(BF16)
        send(qs.at[dq - 1], qr.at[dq - 1], qs_sem.at[dq - 1], qr_sem.at[dq - 1], dev_b(0, dq))
    for dp in range(4):
        qo[dp] = unit(dp, 0)
    text_batch(1)
    ring("L4")
    text_batch(2)
    ring("L3", "S3")
    for i in (0, 2, 1):
        arrived(qr.at[i], qr_sem.at[i])

    def mine(dp):
        return qo[dp] + (qr[0, dp].astype(F32) + qr[1, dp].astype(F32) + qr[2, dp].astype(F32))

    for dp in (2, 1, 3):
        ps[dp - 1] = mine(dp).astype(BF16)
        send(ps.at[dp - 1], pr.at[dp - 1], ts_sem.at[dp - 1], tr_sem.at[dp - 1], dev_b(dp, 0))
    own = mine(0)
    ring("L2", "S2")
    for i in (0, 2, 1):
        arrived(pr.at[i], tr_sem.at[i])
        own = own + pr[i].astype(F32)
    fz[...] = own
    for tz in range(NZ):
        piece = fz[18 * tz : 18 * tz + 18, :]
        zf[tz, :18] = piece
        zs[tz, :18] = piece.astype(BF16)
    for dz in (4, 3, 5, 2, 6, 1, 7):
        send(zs.at[(z + dz) % NZ], zr.at[NZ - dz], zs_sem.at[dz], zr_sem.at[NZ - dz], dev(dz=dz))
    ring("L1", "S1")

    handed("0")
    for c in range(n_chunk):
        dtext_out[c * chunk : (c + 1) * chunk] = gathered("0", c)
    loss = loss_send[ROW_OF_DQ[0] * 4]
    for i in range(1, 16):
        arrived(loss_recv.at[i], l_recv.at[i])
        loss = loss + loss_recv[i]
    loss_out[...] = loss
    outputs = [
        pltpu.make_async_copy(src, dst, out_sem.at[i])
        for i, (src, dst) in enumerate(((loss_out, loss_hbm), (dtext_out, dtext_hbm), (dproj_out, dproj_hbm)))
    ]
    outputs[0].start()
    outputs[1].start()
    acc = zf[z, :18]
    for dz in range(1, 8):
        arrived(zr.at[dz], zr_sem.at[dz])
        acc = acc + zr[dz, :18].astype(F32)
    fin[:18] = acc
    for n in range(4):
        @pl.when(narrow == n)
        def _():
            dproj_out[...] = fin[:18, 32 * n : 32 * n + 288]

    outputs[2].start()
    for copy in sends:
        copy.wait_send()
    for i in range(7):
        sent(rsend.at[i], rs_sem.at[i])
    sent(ta.at[pl.ds(0, 15 * rows)], a_send)
    sent(ub.at[pl.ds(0, 15 * rows)], b_send)
    sent(fb.at[pl.ds(0, 15 * rows)], f_send)
    sent(loss_send.at[pl.ds(0, 15)], l_send)
    for copy in outputs:
        copy.wait()


def results(loss_ref, dtext_ref, dproj_ref, loss_out, dtext_out, dproj_out):
    loss_out[...] = loss_ref[:1, : loss_out.shape[1]]
    dtext_out[...] = dtext_ref[...]
    dproj_out[...] = dproj_ref[...]


def local(image_feats, proj_weight, text_embed, log_scale, logit_bias):
    rows, width = image_feats.shape
    vmem = pl.BlockSpec(memory_space=pltpu.VMEM)
    anywhere = pl.BlockSpec(memory_space=pl.ANY)
    group = 16 * rows
    dma = pltpu.SemaphoreType.DMA
    loss, d_text, d_proj = pl.pallas_call(
        kernel,
        out_shape=(
            jax.ShapeDtypeStruct((8, 128), F32),
            jax.ShapeDtypeStruct((rows, width), F32),
            jax.ShapeDtypeStruct((width // 64, width // 4), F32),
        ),
        in_specs=[anywhere] * 5,
        out_specs=(anywhere, anywhere, anywhere),
        scratch_shapes=[
            pltpu.SMEM((1,), F32),
            pltpu.SMEM((1,), F32),
            pltpu.VMEM((rows, width), BF16),
            pltpu.VMEM((rows, width), BF16),
            pltpu.VMEM((width, width), BF16),
            pltpu.VMEM((group, width), BF16),
            pltpu.VMEM((group, width), BF16),
            pltpu.VMEM((group, width + 128), BF16),
            pltpu.VMEM((2, group, group // 2), BF16),
            pltpu.VMEM((2, 8, group // 2), F32),
            pltpu.VMEM((16, 8, 128), F32),
            pltpu.VMEM((16, 8, 128), F32),
            pltpu.VMEM((group, width), F32),
            pltpu.VMEM((8, rows, width), BF16),
            pltpu.VMEM((8, rows, width), BF16),
            pltpu.VMEM((7, rows, width), BF16),
            pltpu.VMEM((7, rows, width), BF16),
            pltpu.VMEM((group, width), BF16),
            pltpu.VMEM((width, width), F32),
            pltpu.VMEM((width, width), BF16),
            pltpu.VMEM((2, width, 384), BF16),
            pltpu.VMEM((3, 4, 144, 384), BF16),
            pltpu.VMEM((4, 144, 384), F32),
            pltpu.VMEM((3, 4, 144, 384), BF16),
            pltpu.VMEM((3, 144, 384), BF16),
            pltpu.VMEM((3, 144, 384), BF16),
            pltpu.VMEM((144, 384), F32),
            pltpu.VMEM((8, 24, 384), F32),
            pltpu.VMEM((8, 32, 384), BF16),
            pltpu.VMEM((8, 32, 384), BF16),
            pltpu.VMEM((24, 384), F32),
            pltpu.VMEM((8, 128), F32),
            pltpu.VMEM((rows, width), F32),
            pltpu.VMEM((width // 64, width // 4), F32),
            dma((5,)), dma((3,)), dma, dma((8, 3)), dma((8, 3)),
            dma, dma((16, 3)), dma, dma((16, 1)),
            dma, dma((16,)), dma((8,)), dma((8,)), dma((7,)), dma((7, 3)),
            dma((3, 2)), dma((3, 2)),
            dma((3,)), dma((3,)), dma((3,)), dma((3,)), dma((8,)), dma((8,)),
        ],
        compiler_params=pltpu.CompilerParams(
            collective_id=0, has_side_effects=True, vmem_limit_bytes=60 * 1024 * 1024
        ),
    )(log_scale, logit_bias, image_feats, proj_weight, text_embed)
    loss, d_text, d_proj = pl.pallas_call(
        results,
        out_shape=(
            jax.ShapeDtypeStruct((1, rows), F32),
            jax.ShapeDtypeStruct(d_text.shape, F32),
            jax.ShapeDtypeStruct(d_proj.shape, F32),
        ),
        in_specs=[vmem, vmem, vmem],
        out_specs=(vmem, vmem, vmem),
    )(loss, d_text, d_proj)
    return loss.reshape(rows), d_text, d_proj


def solution(mesh):
    placed = (P(("wide", "narrow"), None), P(), P(("wide", "narrow"), None), P(), P())
    return jax.shard_map(
        local,
        mesh=mesh,
        in_specs=placed,
        out_specs=(P(("wide", "narrow")), P(("wide", "narrow"), None), P("wide", "narrow")),
        check_vma=False,
    )
```

time: 1900 us -> 82.2 us (0.04)
  waiting for transfers between devices: 1350 us -> 0 us
  matrix products: 359 us -> 0 us
  local copies, waits for them, and re-layouts: 105 us -> 0 us
  Pallas kernels: 0 us -> 80.1 us
  blocking collectives: 58 us -> 0 us
    unnamed x4 -> x0, waiting for transfers between devices: 660 us -> none
    ppermute x127 -> x0, waiting for transfers between devices: 659 us -> none  [passed_along(): return lax.ppermute(value, axis, pairs)]
    dot_general x194 -> x0, matrix products: 359 us -> none  [the longest x65 133 us: transposed_product(): lax.dot_general(grad_tile, group_img, (((0,), (0,)), ((), ())), preferred...]
    while x63 -> x0, local copies, waits for them, and re-layouts: 96.9 us -> none
    pallas_call x0 -> x2, Pallas kernels: none -> 80.1 us  [the longest x1 78.4 us: local(): pl.pallas_call(kernel, out_shape=(jax.ShapeDtypeStruct((8, 128), F32), ja...]
    unnamed x1 -> x0, blocking collectives: 48.2 us -> none
    reduce_scatter x2 -> x0, waiting for transfers between devices: 29.7 us -> none  [the longest x1 18.5 us: local(): lax.psum_scatter(d_img, 'narrow', scatter_dimension=0, tiled=True)]
  transfers between devices with their start and end apart: 130 -> 0, of which waited for: 129 -> 0; matrix products, arithmetic and copies ran while one was open for 19% -> 0% of each run, Pallas kernels for 0% -> 0%
where the time goes in v3:
time: 82.2 us; the launch traced here: 82 us
  Pallas kernels  80.1 us (97%)
  between operations  1.93 us (2%)
    pallas_call x1, Pallas kernels, local(): pl.pallas_call(kernel, out_shape=(jax.ShapeDtypeStruct((8, 128), F32), ja...  78.4 us
    pallas_call x1, Pallas kernels, local(): pl.pallas_call(results, out_shape=(jax.ShapeDtypeStruct((1, rows), F32),...  1.65 us

profile of v3, /device:TPU:1, one launch (start us, length us, event | category | flops | bytes accessed | tf_op | source)
XLA Modules:
  0.0 82.0 jit_solution(10167212702346087828)
XLA Ops:
  1.9 78.4 %shard_map.76 = (f32[8,128]{1,0:T(8,128)}, f32[48,1152]{1,0:T(8,128)}, f32[18,288]{1,0:T(8,128)}) custom-call(f32[1]{0:T(128)S(6)} %copy.8.scale_hbm, f32[1]{0:T(128)S(6)} %copy.9.shift_hbm, bf16[48,1152]{1,0:T(8,128)(2,1)} %feats_hbm.1, bf16[1152,1152]{1,0:T(8,128)(2,1)} %w_hbm.1, bf16[48,1152]{1,0:T(8,128)(2,1)} %text_hbm.1), custom_call_target="tpu_custom_call" | custom-call | tf_op jit(solution)/shard_map/pallas_call | solution.py:449
  80.4 1.6 %shard_map.77 = (f32[1,48]{1,0:T(1,128)}, f32[48,1152]{1,0:T(8,128)}, f32[18,288]{1,0:T(8,128)}) custom-call(f32[8,128]{1,0:T(8,128)} %get-tuple-element.9.loss_ref, f32[48,1152]{1,0:T(8,128)} %get-tuple-element.10.dtext_ref, f32[18,288]{1,0:T(8,128)} %get-tuple-element.11.dproj_ref), custom_call_target="tpu_custom_call" | custom-call | tf_op jit(solution)/shard_map/pallas_call | solution.py:503

commit v4 on v3

--- a/solution.py
+++ b/solution.py
@@ -27,10 +27,10 @@
 def kernel(
     scale_hbm, shift_hbm, feats_hbm, w_hbm, text_hbm,
     loss_hbm, dtext_hbm, dproj_hbm,
-    scale_ref, shift_ref, feats_ref, text_ref, wv, ta, ub, fb, g, loss_acc, loss_send, loss_recv,
+    scale_ref, shift_ref, feats_ref, text_ref, wv, order, wp, ta, ub, fb, inv, g, loss_acc, loss_send, loss_recv,
     d_text, psend, precv, rsend, rrecv, dzb, qf, qb, pq, qs, qo, qr, ps, pr, fz, zf, zs, zr, fin,
     loss_out, dtext_out, dproj_out,
-    in_sem, out_sem, a_send, a_ring_recv, a_part_recv, b_send, b_recv, f_send, f_recv,
+    in_sem, out_sem, a_send, a_ring_recv, a_part_recv, b_send, b_recv,
     l_send, l_recv, ps_sem, pr_sem, rs_sem, rr_sem, pq_send, pq_recv,
     qs_sem, qr_sem, ts_sem, tr_sem, zs_sem, zr_sem,
 ):
@@ -179,16 +179,19 @@
             self.wait(0, 3, c)
             self.wait(1, 3, c)
 
+        def fourth(self, c):
+            self.wait(3, 1, c)
+            self.wait(2, 1, c)
+
         def last(self, c):
-            for dp, dq in ((3, 1), (2, 1), (0, 2), (3, 2), (1, 2), (2, 2)):
+            for dp, dq in ((0, 2), (3, 2), (1, 2), (2, 2)):
                 self.wait(dp, dq, c)
 
         def run(self, step):
             for c in range(rows // self.size):
                 step(c)
 
-    images = Plane(ub, b_send, b_recv, chunk)
-    feats = Plane(fb, f_send, f_recv, rows)
+    images = Plane(fb, b_send, b_recv, chunk)
 
     inputs[0].wait()
     text = text_ref[...].astype(F32)
@@ -196,32 +199,43 @@
     own_a = SLOT_ROW[("O", "0")] * rows
     own_b = ROW_OF_DQ[0] * 4 * rows
     ta[own_a : own_a + rows] = (text * text_inv).astype(BF16)
-    inputs[1].wait()
-    zs[...] = jnp.zeros_like(zs)
-    loss_send[...] = jnp.zeros_like(loss_send)
-
-    pl.semaphore_wait(barrier, len(peers))
-    a_start()
-
-    for copy in inputs[2:]:
-        copy.wait()
-    zproj = jnp.dot(feats_ref[...], wv[...], preferred_element_type=F32)
-    img_inv = lax.rsqrt(jnp.sum(zproj * zproj, axis=1, keepdims=True) + 1e-06)
-    ub[own_b : own_b + rows] = (zproj * img_inv).astype(BF16)
-    images.run(images.start)
-
-    col = lax.broadcasted_iota(jnp.int32, (8, width), 1)
+
+    col = lax.broadcasted_iota(jnp.int32, (width, 128), 0)
     combo = (col * 911) >> 17
     rest = col - 144 * combo
     layer = (rest * 3641) >> 16
     source = 18 * (32 * (combo >> 2) + 4 * layer + (combo & 3)) + rest - 18 * layer
-    order = jnp.where(lax.broadcasted_iota(jnp.int32, (width, width), 0) == source[:1], 1.0, 0.0).astype(BF16)
-    fb[own_b : own_b + rows, :width] = jnp.dot(feats_ref[...], order, preferred_element_type=F32).astype(BF16)
-    lane = lax.broadcasted_iota(jnp.int32, (rows, 128), 1)
-    inv_hi = img_inv.astype(BF16).astype(F32)
-    fb[own_b : own_b + rows, width:] = jnp.where(
-        lane == 0, inv_hi, jnp.where(lane == 1, img_inv - inv_hi, 0.0)
+    lane = lax.broadcasted_iota(jnp.int32, (width, 128), 1)
+    for j in range(width // 128):
+        order[:, 128 * j : 128 * (j + 1)] = jnp.where(source == lane + 128 * j, 1.0, 0.0).astype(BF16)
+    inputs[1].wait()
+    fb[own_b : own_b + rows] = lax.dot_general(
+        feats_ref[...], order[...], (((1,), (1,)), ((), ())), preferred_element_type=F32
     ).astype(BF16)
+    zs[...] = jnp.zeros_like(zs)
+    loss_send[...] = jnp.zeros_like(loss_send)
+
+    def weight(b):
+        r = slice(384 * b, 384 * (b + 1))
+        wp[r, :] = jnp.dot(order[r, :], wv[...], preferred_element_type=F32).astype(BF16)
+
+    for copy in inputs[2:]:
+        copy.wait()
+    weight(0)
+    pl.semaphore_wait(barrier, len(peers))
+    a_start()
+    images.run(images.start)
+    weight(1)
+    weight(2)
+
+    quarter = 4 * rows
+
+    def project(dq):
+        r = slice(ROW_OF_DQ[dq] * quarter, (ROW_OF_DQ[dq] + 1) * quarter)
+        zproj = jnp.dot(fb[r, :], wp[...], preferred_element_type=F32)
+        img_inv = lax.rsqrt(jnp.sum(zproj * zproj, axis=1, keepdims=True) + 1e-06)
+        ub[r, :] = (zproj * img_inv).astype(BF16)
+        inv[r, :] = jnp.broadcast_to(img_inv, (quarter, 128))
 
     scale = jnp.exp(jnp.full((1, 128), scale_ref[0], F32))[:, :1]
     shift = shift_ref[0]
@@ -254,18 +268,21 @@
     images.run(images.first)
     a_step(2)
     images.run(images.second)
+    project(0)
     a_step(3)
     images.run(images.third)
+    project(3)
+    a_step(4)
+    images.run(images.fourth)
     a_finish("0", "L1", "S1")
     cell(2, 1)
-    a_step(4)
-    feats.run(feats.start)
+    project(1)
     a_finish("L2", "S2")
     cell(1, 1)
     images.run(images.last)
+    project(2)
     cell(2, 0)
     cell(1, 0)
-    feats.run(feats.first)
     a_finish("L3", "S3", "L4")
     cell(0, 1)
     cell(0, 0)
@@ -274,8 +291,7 @@
         r = slice(pair * half, (pair + 1) * half)
         d = lax.dot_general(g[pair], ta[...], (((0,), (0,)), ((), ())), preferred_element_type=F32)
         u = ub[r, :].astype(F32)
-        factor = jnp.sum(fb[r, width:].astype(F32), axis=1, keepdims=True)
-        dzb[r, :] = (factor * (d - u * jnp.sum(u * d, axis=1, keepdims=True))).astype(BF16)
+        dzb[r, :] = (inv[r, :1] * (d - u * jnp.sum(u * d, axis=1, keepdims=True))).astype(BF16)
 
     for pair in range(2):
         summed = jnp.sum(loss_acc[pair], axis=0, keepdims=True)
@@ -288,9 +304,6 @@
                 k = ROW_OF_DQ[dq] * 4 + dp
                 send(loss_send.at[k], loss_recv.at[i], l_send, l_recv.at[i], dev_b(dp, dq), keep=False)
 
-    feats.run(feats.second)
-    feats.run(feats.third)
-    feats.run(feats.last)
     image_half(1)
     image_half(0)
 
@@ -364,39 +377,35 @@
     for b in range(width // block):
         for yl in range(2):
             arrived(pq.at[yl, pl.ds(b * block, block)], pq_recv.at[b, yl])
-    for dq in (2, 1, 3):
-        for dp in range(4):
+    for dp in (2, 1, 3, 0):
+        for dq in (2, 1, 3):
             qs[dq - 1, dp] = unit(dp, dq).astype(BF16)
-        send(qs.at[dq - 1], qr.at[dq - 1], qs_sem.at[dq - 1], qr_sem.at[dq - 1], dev_b(0, dq))
+            send(
+                qs.at[dq - 1, dp], qr.at[dq - 1, dp], qs_sem.at[dq - 1, dp], qr_sem.at[dq - 1, dp], dev_b(0, dq)
+            )
     for dp in range(4):
         qo[dp] = unit(dp, 0)
     text_batch(1)
     ring("L4")
     text_batch(2)
     ring("L3", "S3")
-    for i in (0, 2, 1):
-        arrived(qr.at[i], qr_sem.at[i])
+    ring("L2", "S2")
 
     def mine(dp):
-        return qo[dp] + (qr[0, dp].astype(F32) + qr[1, dp].astype(F32) + qr[2, dp].astype(F32))
-
-    for dp in (2, 1, 3):
+        total = qo[dp]
+        for i in (0, 2, 1):
+            arrived(qr.at[i, dp], qr_sem.at[i, dp])
+            total = total + qr[i, dp].astype(F32)
+        return total
+
+    def plane(dp):
         ps[dp - 1] = mine(dp).astype(BF16)
         send(ps.at[dp - 1], pr.at[dp - 1], ts_sem.at[dp - 1], tr_sem.at[dp - 1], dev_b(dp, 0))
-    own = mine(0)
-    ring("L2", "S2")
-    for i in (0, 2, 1):
-        arrived(pr.at[i], tr_sem.at[i])
-        own = own + pr[i].astype(F32)
-    fz[...] = own
-    for tz in range(NZ):
-        piece = fz[18 * tz : 18 * tz + 18, :]
-        zf[tz, :18] = piece
-        zs[tz, :18] = piece.astype(BF16)
-    for dz in (4, 3, 5, 2, 6, 1, 7):
-        send(zs.at[(z + dz) % NZ], zr.at[NZ - dz], zs_sem.at[dz], zr_sem.at[NZ - dz], dev(dz=dz))
+
+    plane(2)
     ring("L1", "S1")
-
+    plane(1)
+    plane(3)
     handed("0")
     for c in range(n_chunk):
         dtext_out[c * chunk : (c + 1) * chunk] = gathered("0", c)
@@ -411,6 +420,18 @@
     ]
     outputs[0].start()
     outputs[1].start()
+    own = mine(0)
+    for i in (0, 2, 1):
+        arrived(pr.at[i], tr_sem.at[i])
+        own = own + pr[i].astype(F32)
+    fz[...] = own
+    for tz in range(NZ):
+        piece = fz[18 * tz : 18 * tz + 18, :]
+        zf[tz, :18] = piece
+        zs[tz, :18] = piece.astype(BF16)
+    for dz in (4, 3, 5, 2, 6, 1, 7):
+        send(zs.at[(z + dz) % NZ], zr.at[NZ - dz], zs_sem.at[dz], zr_sem.at[NZ - dz], dev(dz=dz))
+
     acc = zf[z, :18]
     for dz in range(1, 8):
         arrived(zr.at[dz], zr_sem.at[dz])
@@ -427,8 +448,7 @@
     for i in range(7):
         sent(rsend.at[i], rs_sem.at[i])
     sent(ta.at[pl.ds(0, 15 * rows)], a_send)
-    sent(ub.at[pl.ds(0, 15 * rows)], b_send)
-    sent(fb.at[pl.ds(0, 15 * rows)], f_send)
+    sent(fb.at[pl.ds(0, 15 * rows)], b_send)
     sent(loss_send.at[pl.ds(0, 15)], l_send)
     for copy in outputs:
         copy.wait()
@@ -461,9 +481,12 @@
             pltpu.VMEM((rows, width), BF16),
             pltpu.VMEM((rows, width), BF16),
             pltpu.VMEM((width, width), BF16),
+            pltpu.VMEM((width, width), BF16),
+            pltpu.VMEM((width, width), BF16),
             pltpu.VMEM((group, width), BF16),
             pltpu.VMEM((group, width), BF16),
-            pltpu.VMEM((group, width + 128), BF16),
+            pltpu.VMEM((group, width), BF16),
+            pltpu.VMEM((group, 128), F32),
             pltpu.VMEM((2, group, group // 2), BF16),
             pltpu.VMEM((2, 8, group // 2), F32),
             pltpu.VMEM((16, 8, 128), F32),
@@ -491,10 +514,10 @@
             pltpu.VMEM((rows, width), F32),
             pltpu.VMEM((width // 64, width // 4), F32),
             dma((5,)), dma((3,)), dma, dma((8, 3)), dma((8, 3)),
-            dma, dma((16, 3)), dma, dma((16, 1)),
+            dma, dma((16, 3)),
             dma, dma((16,)), dma((8,)), dma((8,)), dma((7,)), dma((7, 3)),
             dma((3, 2)), dma((3, 2)),
-            dma((3,)), dma((3,)), dma((3,)), dma((3,)), dma((8,)), dma((8,)),
+            dma((3, 4)), dma((3, 4)), dma((3,)), dma((3,)), dma((8,)), dma((8,)),
         ],
         compiler_params=pltpu.CompilerParams(
             collective_id=0, has_side_effects=True, vmem_limit_bytes=60 * 1024 * 1024

time: 82.2 us -> 67.8 us (0.82)
  the two profiles are of different devices: /device:TPU:1 before, /device:TPU:8 now
where the time goes in v4:
time: 67.8 us; the launch traced here: 67.7 us
  Pallas kernels  65.8 us (97%)
  between operations  1.93 us (3%)
    pallas_call x1, Pallas kernels, local(): pl.pallas_call(kernel, out_shape=(jax.ShapeDtypeStruct((8, 128), F32), ja...  64.1 us
    pallas_call x1, Pallas kernels, local(): pl.pallas_call(results, out_shape=(jax.ShapeDtypeStruct((1, rows), F32),...  1.65 us

profile of v4, /device:TPU:8, one launch (start us, length us, event | category | flops | bytes accessed | tf_op | source)
XLA Modules:
  0.0 67.7 jit_solution(5162425740989779918)
XLA Ops:
  1.9 64.1 %shard_map.76 = (f32[8,128]{1,0:T(8,128)}, f32[48,1152]{1,0:T(8,128)}, f32[18,288]{1,0:T(8,128)}) custom-call(f32[1]{0:T(128)S(6)} %copy.8.scale_hbm, f32[1]{0:T(128)S(6)} %copy.9.shift_hbm, bf16[48,1152]{1,0:T(8,128)(2,1)} %feats_hbm.1, bf16[1152,1152]{1,0:T(8,128)(2,1)} %w_hbm.1, bf16[48,1152]{1,0:T(8,128)(2,1)} %text_hbm.1), custom_call_target="tpu_custom_call" | custom-call | tf_op jit(solution)/shard_map/pallas_call | solution.py:469
  66.0 1.6 %shard_map.77 = (f32[1,48]{1,0:T(1,128)}, f32[48,1152]{1,0:T(8,128)}, f32[18,288]{1,0:T(8,128)}) custom-call(f32[8,128]{1,0:T(8,128)} %get-tuple-element.9.loss_ref, f32[48,1152]{1,0:T(8,128)} %get-tuple-element.10.dtext_ref, f32[18,288]{1,0:T(8,128)} %get-tuple-element.11.dproj_ref), custom_call_target="tpu_custom_call" | custom-call | tf_op jit(solution)/shard_map/pallas_call | solution.py:526

commit v5 on v4

--- a/solution.py
+++ b/solution.py
@@ -21,14 +21,18 @@
 SLOT_ROW = {name: i for i, name in enumerate(SLOTS)}
 BATCHES = ((0, 6), (6, 10), (10, 16))
 RING = STREAM[:7]
-ROW_OF_DQ = {2: 0, 1: 1, 0: 2, 3: 3}
+PLANE_SLOTS = (
+    (3, 1), (1, 3), (0, 2), (2, 3), (2, 1), (3, 2), (1, 2), (2, 2),
+    (0, 0), (3, 0), (1, 0), (0, 1), (0, 3), (2, 0), (3, 3), (1, 1),
+)
+PLANE_ROW = {slot: i for i, slot in enumerate(PLANE_SLOTS)}
 
 
 def kernel(
     scale_hbm, shift_hbm, feats_hbm, w_hbm, text_hbm,
     loss_hbm, dtext_hbm, dproj_hbm,
     scale_ref, shift_ref, feats_ref, text_ref, wv, order, wp, ta, ub, fb, inv, g, loss_acc, loss_send, loss_recv,
-    d_text, psend, precv, rsend, rrecv, dzb, qf, qb, pq, qs, qo, qr, ps, pr, fz, zf, zs, zr, fin,
+    d_text, psend, precv, rsend, rrecv, dzb, qf, qb, pq, qs, qo, qr, ps, pr, fz, zf, zs, zr, ext, fin,
     loss_out, dtext_out, dproj_out,
     in_sem, out_sem, a_send, a_ring_recv, a_part_recv, b_send, b_recv,
     l_send, l_recv, ps_sem, pr_sem, rs_sem, rr_sem, pq_send, pq_recv,
@@ -88,8 +92,7 @@
         rcopy(dst, dst, rsem, rsem, partner).wait_recv()
 
     barrier = pltpu.get_barrier_semaphore()
-    peers = [dev_b(dp, dq) for dp in range(4) for dq in range(4) if (dp, dq) != (0, 0)]
-    peers += [dev(dz=dz) for dz in range(1, 8)] + [partner]
+    peers = [dev_b(1, 0), dev_b(3, 0), dev_b(0, 1), dev_b(0, 3), along, against, partner]
     for peer in peers:
         pl.semaphore_signal(barrier, inc=1, device_id=peer, device_id_type=MESH)
 
@@ -102,7 +105,7 @@
 
     def a_hand(name, c):
         i = STREAM.index(name)
-        send(a_part(("O", name), c), a_part(("X", name), c), a_send, a_part_recv.at[i, c], partner, keep=False)
+        send(a_part(("O", name), c), a_part(("X", name), c), a_send, a_part_recv.at[i], partner, keep=False)
 
     def a_start():
         for c in range(n_chunk):
@@ -127,15 +130,14 @@
 
     def a_finish(*names):
         for name in names:
-            for c in range(n_chunk):
-                arrived(a_part(("X", name), c), a_part_recv.at[STREAM.index(name), c])
+            arrived(ta.at[pl.ds(SLOT_ROW["X", name] * rows, rows)], a_part_recv.at[STREAM.index(name)])
 
     class Plane:
         def __init__(self, buf, ssem, rsem, size):
             self.buf, self.ssem, self.rsem, self.size = buf, ssem, rsem, size
 
         def part(self, dp, dq, c):
-            return self.buf.at[pl.ds((ROW_OF_DQ[dq % 4] * 4 + dp % 4) * rows + c * self.size, self.size)]
+            return self.buf.at[pl.ds(PLANE_ROW[dp % 4, dq % 4] * rows + c * self.size, self.size)]
 
         def copy(self, dp, dq, mp, mq, c):
             to = ((dp - mp) % 4, (dq - mq) % 4)
@@ -176,29 +178,17 @@
         def third(self, c):
             self.wait(2, 3, c)
             self.copy(2, 3, 0, 1, c)
-            self.wait(0, 3, c)
-            self.wait(1, 3, c)
-
-        def fourth(self, c):
-            self.wait(3, 1, c)
-            self.wait(2, 1, c)
-
-        def last(self, c):
-            for dp, dq in ((0, 2), (3, 2), (1, 2), (2, 2)):
-                self.wait(dp, dq, c)
+
+        def last(self, *slots):
+            for c in range(rows // self.size):
+                for dp, dq in slots:
+                    self.wait(dp, dq, c)
 
         def run(self, step):
             for c in range(rows // self.size):
                 step(c)
 
     images = Plane(fb, b_send, b_recv, chunk)
-
-    inputs[0].wait()
-    text = text_ref[...].astype(F32)
-    text_inv = lax.rsqrt(jnp.sum(text * text, axis=1, keepdims=True) + 1e-06)
-    own_a = SLOT_ROW[("O", "0")] * rows
-    own_b = ROW_OF_DQ[0] * 4 * rows
-    ta[own_a : own_a + rows] = (text * text_inv).astype(BF16)
 
     col = lax.broadcasted_iota(jnp.int32, (width, 128), 0)
     combo = (col * 911) >> 17
@@ -208,11 +198,22 @@
     lane = lax.broadcasted_iota(jnp.int32, (width, 128), 1)
     for j in range(width // 128):
         order[:, 128 * j : 128 * (j + 1)] = jnp.where(source == lane + 128 * j, 1.0, 0.0).astype(BF16)
+    inputs[0].wait()
+    text = text_ref[...].astype(F32)
+    text_inv = lax.rsqrt(jnp.sum(text * text, axis=1, keepdims=True) + 1e-06)
+    own_a = SLOT_ROW[("O", "0")] * rows
+    own_b = PLANE_ROW[0, 0] * rows
+    ta[own_a : own_a + rows] = (text * text_inv).astype(BF16)
+
+    pl.semaphore_wait(barrier, len(peers))
+    a_start()
     inputs[1].wait()
     fb[own_b : own_b + rows] = lax.dot_general(
         feats_ref[...], order[...], (((1,), (1,)), ((), ())), preferred_element_type=F32
     ).astype(BF16)
+    images.run(images.start)
     zs[...] = jnp.zeros_like(zs)
+    ext[...] = jnp.zeros_like(ext)
     loss_send[...] = jnp.zeros_like(loss_send)
 
     def weight(b):
@@ -222,25 +223,19 @@
     for copy in inputs[2:]:
         copy.wait()
     weight(0)
-    pl.semaphore_wait(barrier, len(peers))
-    a_start()
-    images.run(images.start)
     weight(1)
-    weight(2)
-
-    quarter = 4 * rows
-
-    def project(dq):
-        r = slice(ROW_OF_DQ[dq] * quarter, (ROW_OF_DQ[dq] + 1) * quarter)
+
+    half = 8 * rows
+
+    def project(lo, hi):
+        r = slice(lo * rows, hi * rows)
         zproj = jnp.dot(fb[r, :], wp[...], preferred_element_type=F32)
         img_inv = lax.rsqrt(jnp.sum(zproj * zproj, axis=1, keepdims=True) + 1e-06)
         ub[r, :] = (zproj * img_inv).astype(BF16)
-        inv[r, :] = jnp.broadcast_to(img_inv, (quarter, 128))
+        inv[r, :] = jnp.broadcast_to(img_inv, ((hi - lo) * rows, 128))
 
     scale = jnp.exp(jnp.full((1, 128), scale_ref[0], F32))[:, :1]
     shift = shift_ref[0]
-    half = 8 * rows
-
     def cell(batch, pair):
         r0, r1 = (rows * b for b in BATCHES[batch])
         prod = lax.dot_general(
@@ -264,23 +259,25 @@
             else:
                 loss_acc[pair, :, lanes] += total
 
+    images.run(images.first)
     a_step(1)
-    images.run(images.first)
+    weight(2)
+    images.last((0, 3))
+    project(8, 13)
+    images.run(images.second)
     a_step(2)
-    images.run(images.second)
-    project(0)
+    project(13, 16)
+    a_finish("0", "L1", "S1")
+    cell(2, 1)
     a_step(3)
     images.run(images.third)
-    project(3)
-    a_step(4)
-    images.run(images.fourth)
-    a_finish("0", "L1", "S1")
-    cell(2, 1)
-    project(1)
     a_finish("L2", "S2")
     cell(1, 1)
-    images.run(images.last)
-    project(2)
+    images.last((3, 1), (1, 3), (0, 2))
+    project(0, 3)
+    a_step(4)
+    images.last((2, 1), (3, 2), (1, 2), (2, 2))
+    project(3, 8)
     cell(2, 0)
     cell(1, 0)
     a_finish("L3", "S3", "L4")
@@ -297,12 +294,10 @@
         summed = jnp.sum(loss_acc[pair], axis=0, keepdims=True)
         for k in range(8):
             loss_send[8 * pair + k, :1, :rows] = summed[:, k * rows : (k + 1) * rows]
-    for dq in range(4):
-        for dp in range(4):
-            if (dp, dq) != (0, 0):
-                i = ((4 - dq) % 4) * 4 + (4 - dp) % 4
-                k = ROW_OF_DQ[dq] * 4 + dp
-                send(loss_send.at[k], loss_recv.at[i], l_send, l_recv.at[i], dev_b(dp, dq), keep=False)
+    for k, (dp, dq) in enumerate(PLANE_SLOTS):
+        if (dp, dq) != (0, 0):
+            i = ((4 - dq) % 4) * 4 + (4 - dp) % 4
+            send(loss_send.at[k], loss_recv.at[i], l_send, l_recv, dev_b(dp, dq), keep=False)
 
     image_half(1)
     image_half(0)
@@ -315,7 +310,7 @@
         qb[r, :] = out.astype(BF16)
         for yl in range(2):
             lanes = pl.ds(pl.multiple_of(256 * (1 - core) + 512 * yl, 128), 384)
-            send(qb.at[r, lanes], pq.at[yl, r], pq_send.at[b, yl], pq_recv.at[b, yl], partner)
+            send(qb.at[r, lanes], pq.at[yl, r], pq_send, pq_recv, partner, keep=False)
 
     def slot_rows(slot, c=None):
         if c is None:
@@ -332,7 +327,7 @@
             if kind == "X":
                 i = STREAM.index(name)
                 psend[i] = d_text[slot_rows((kind, name)), :].astype(BF16)
-                send(psend.at[i], precv.at[i], ps_sem.at[i], pr_sem.at[i], partner)
+                send(psend.at[i], precv.at[i], ps_sem, pr_sem.at[i], partner, keep=False)
 
     def handed(name):
         i = STREAM.index(name)
@@ -362,7 +357,7 @@
                 i = RING.index(name)
                 rsend[i, r] = gathered(name, c).astype(BF16)
                 send(
-                    rsend.at[i, r], rrecv.at[i, r], rs_sem.at[i], rr_sem.at[i, c],
+                    rsend.at[i, r], rrecv.at[i, r], rs_sem, rr_sem.at[i, c],
                     against if name[0] == "L" else along, keep=False,
                 )
 
@@ -374,14 +369,12 @@
         return qf[r, lanes] + pq[py % 2, r, :].astype(F32)
 
     text_batch(0)
-    for b in range(width // block):
-        for yl in range(2):
-            arrived(pq.at[yl, pl.ds(b * block, block)], pq_recv.at[b, yl])
+    arrived(pq, pq_recv)
     for dp in (2, 1, 3, 0):
         for dq in (2, 1, 3):
             qs[dq - 1, dp] = unit(dp, dq).astype(BF16)
             send(
-                qs.at[dq - 1, dp], qr.at[dq - 1, dp], qs_sem.at[dq - 1, dp], qr_sem.at[dq - 1, dp], dev_b(0, dq)
+                qs.at[dq - 1, dp], qr.at[dq - 1, dp], qs_sem, qr_sem.at[dq - 1, dp], dev_b(0, dq), keep=False,
             )
     for dp in range(4):
         qo[dp] = unit(dp, 0)
@@ -389,7 +382,6 @@
     ring("L4")
     text_batch(2)
     ring("L3", "S3")
-    ring("L2", "S2")
 
     def mine(dp):
         total = qo[dp]
@@ -400,18 +392,34 @@
 
     def plane(dp):
         ps[dp - 1] = mine(dp).astype(BF16)
-        send(ps.at[dp - 1], pr.at[dp - 1], ts_sem.at[dp - 1], tr_sem.at[dp - 1], dev_b(dp, 0))
+        send(ps.at[dp - 1], pr.at[dp - 1], ts_sem, tr_sem, dev_b(dp, 0), keep=False)
 
     plane(2)
-    ring("L1", "S1")
+    ring("L2", "S2")
     plane(1)
     plane(3)
+    ring("L1", "S1")
+    own = mine(0)
+    arrived(pr, tr_sem)
+    for i in (0, 2, 1):
+        own = own + pr[i].astype(F32)
+    fz[...] = own
+    for tz in range(NZ):
+        piece = fz[18 * tz : 18 * tz + 18, :]
+        zf[tz, :18] = piece
+        zs[tz, :, :384] = piece[:16].astype(BF16)
+        for t in range(3):
+            ext[2 * t : 2 * t + 2, :] = fz[18 * tz + 16 : 18 * tz + 18, 128 * t : 128 * (t + 1)]
+        zs[tz, :, 384:] = ext[...].astype(BF16)
+    for dz in (4, 3, 5, 2, 6, 1, 7):
+        send(zs.at[(z + dz) % NZ], zr.at[NZ - dz], zs_sem, zr_sem, dev(dz=dz), keep=False)
+
     handed("0")
     for c in range(n_chunk):
         dtext_out[c * chunk : (c + 1) * chunk] = gathered("0", c)
-    loss = loss_send[ROW_OF_DQ[0] * 4]
+    loss = loss_send[PLANE_ROW[0, 0]]
+    arrived(loss_recv.at[pl.ds(1, 15)], l_recv)
     for i in range(1, 16):
-        arrived(loss_recv.at[i], l_recv.at[i])
         loss = loss + loss_recv[i]
     loss_out[...] = loss
     outputs = [
@@ -420,23 +428,13 @@
     ]
     outputs[0].start()
     outputs[1].start()
-    own = mine(0)
-    for i in (0, 2, 1):
-        arrived(pr.at[i], tr_sem.at[i])
-        own = own + pr[i].astype(F32)
-    fz[...] = own
-    for tz in range(NZ):
-        piece = fz[18 * tz : 18 * tz + 18, :]
-        zf[tz, :18] = piece
-        zs[tz, :18] = piece.astype(BF16)
-    for dz in (4, 3, 5, 2, 6, 1, 7):
-        send(zs.at[(z + dz) % NZ], zr.at[NZ - dz], zs_sem.at[dz], zr_sem.at[NZ - dz], dev(dz=dz))
-
-    acc = zf[z, :18]
+    acc = jnp.zeros((16, 512), F32)
+    arrived(zr.at[pl.ds(1, 7)], zr_sem)
     for dz in range(1, 8):
-        arrived(zr.at[dz], zr_sem.at[dz])
-        acc = acc + zr[dz, :18].astype(F32)
-    fin[:18] = acc
+        acc = acc + zr[dz].astype(F32)
+    fin[:16] = zf[z, :16] + acc[:, :384]
+    for t in range(3):
+        fin[16:18, 128 * t : 128 * (t + 1)] = zf[z, 16:18, 128 * t : 128 * (t + 1)] + acc[2 * t : 2 * t + 2, 384:]
     for n in range(4):
         @pl.when(narrow == n)
         def _():
@@ -445,8 +443,9 @@
     outputs[2].start()
     for copy in sends:
         copy.wait_send()
-    for i in range(7):
-        sent(rsend.at[i], rs_sem.at[i])
+    for buf, ssem in ((rsend, rs_sem), (psend, ps_sem), (qs, qs_sem), (ps, ts_sem), (pq, pq_send)):
+        sent(buf, ssem)
+    sent(zs.at[pl.ds(0, 7)], zs_sem)
     sent(ta.at[pl.ds(0, 15 * rows)], a_send)
     sent(fb.at[pl.ds(0, 15 * rows)], b_send)
     sent(loss_send.at[pl.ds(0, 15)], l_send)
@@ -473,7 +472,7 @@
             jax.ShapeDtypeStruct((rows, width), F32),
             jax.ShapeDtypeStruct((width // 64, width // 4), F32),
         ),
-        in_specs=[anywhere] * 5,
+        in_specs=[pl.BlockSpec(memory_space=pltpu.HBM)] * 5,
         out_specs=(anywhere, anywhere, anywhere),
         scratch_shapes=[
             pltpu.SMEM((1,), F32),
@@ -507,17 +506,18 @@
             pltpu.VMEM((3, 144, 384), BF16),
             pltpu.VMEM((144, 384), F32),
             pltpu.VMEM((8, 24, 384), F32),
-            pltpu.VMEM((8, 32, 384), BF16),
-            pltpu.VMEM((8, 32, 384), BF16),
+            pltpu.VMEM((8, 16, 512), BF16),
+            pltpu.VMEM((8, 16, 512), BF16),
+            pltpu.VMEM((16, 128), F32),
             pltpu.VMEM((24, 384), F32),
             pltpu.VMEM((8, 128), F32),
             pltpu.VMEM((rows, width), F32),
             pltpu.VMEM((width // 64, width // 4), F32),
-            dma((5,)), dma((3,)), dma, dma((8, 3)), dma((8, 3)),
+            dma((5,)), dma((3,)), dma, dma((8, 3)), dma((8,)),
             dma, dma((16, 3)),
-            dma, dma((16,)), dma((8,)), dma((8,)), dma((7,)), dma((7, 3)),
-            dma((3, 2)), dma((3, 2)),
-            dma((3, 4)), dma((3, 4)), dma((3,)), dma((3,)), dma((8,)), dma((8,)),
+            dma, dma, dma, dma((8,)), dma, dma((7, 3)),
+            dma, dma,
+            dma, dma((3, 4)), dma, dma, dma, dma,
         ],
         compiler_params=pltpu.CompilerParams(
             collective_id=0, has_side_effects=True, vmem_limit_bytes=60 * 1024 * 1024

time: 67.8 us -> 64.5 us (0.951)
  the two profiles are of different devices: /device:TPU:8 before, /device:TPU:1 now
where the time goes in v5:
time: 64.5 us; the launch traced here: 64.4 us
  Pallas kernels  62.5 us (97%)
  between operations  1.93 us (3%)
    pallas_call x1, Pallas kernels, local(): pl.pallas_call(kernel, out_shape=(jax.ShapeDtypeStruct((8, 128), F32), ja...  60.9 us
    pallas_call x1, Pallas kernels, local(): pl.pallas_call(results, out_shape=(jax.ShapeDtypeStruct((1, rows), F32),...  1.65 us

profile of v5, /device:TPU:1, one launch (start us, length us, event | category | flops | bytes accessed | tf_op | source)
XLA Modules:
  0.0 64.4 jit_solution(14821121609649839119)
XLA Ops:
  1.9 60.9 %shard_map.76 = (f32[8,128]{1,0:T(8,128)}, f32[48,1152]{1,0:T(8,128)}, f32[18,288]{1,0:T(8,128)}) custom-call(f32[1]{0:T(128)S(6)} %copy.8.scale_hbm, f32[1]{0:T(128)S(6)} %copy.9.shift_hbm, bf16[48,1152]{1,0:T(8,128)(2,1)} %feats_hbm.1, bf16[1152,1152]{1,0:T(8,128)(2,1)} %w_hbm.1, bf16[48,1152]{1,0:T(8,128)(2,1)} %text_hbm.1), custom_call_target="tpu_custom_call" | custom-call | tf_op jit(solution)/shard_map/pallas_call | solution.py:468
  62.8 1.6 %shard_map.77 = (f32[1,48]{1,0:T(1,128)}, f32[48,1152]{1,0:T(8,128)}, f32[18,288]{1,0:T(8,128)}) custom-call(f32[8,128]{1,0:T(8,128)} %get-tuple-element.9.loss_ref, f32[48,1152]{1,0:T(8,128)} %get-tuple-element.10.dtext_ref, f32[18,288]{1,0:T(8,128)} %get-tuple-element.11.dproj_ref), custom_call_target="tpu_custom_call" | custom-call | tf_op jit(solution)/shard_map/pallas_call | solution.py:526

commit v6 on v5

--- a/solution.py
+++ b/solution.py
@@ -259,47 +259,37 @@
             else:
                 loss_acc[pair, :, lanes] += total
 
-    images.run(images.first)
-    a_step(1)
-    weight(2)
-    images.last((0, 3))
-    project(8, 13)
-    images.run(images.second)
-    a_step(2)
-    project(13, 16)
-    a_finish("0", "L1", "S1")
-    cell(2, 1)
-    a_step(3)
-    images.run(images.third)
-    a_finish("L2", "S2")
-    cell(1, 1)
-    images.last((3, 1), (1, 3), (0, 2))
-    project(0, 3)
-    a_step(4)
-    images.last((2, 1), (3, 2), (1, 2), (2, 2))
-    project(3, 8)
-    cell(2, 0)
-    cell(1, 0)
-    a_finish("L3", "S3", "L4")
-    cell(0, 1)
-    cell(0, 0)
-
     def image_half(pair):
         r = slice(pair * half, (pair + 1) * half)
         d = lax.dot_general(g[pair], ta[...], (((0,), (0,)), ((), ())), preferred_element_type=F32)
         u = ub[r, :].astype(F32)
         dzb[r, :] = (inv[r, :1] * (d - u * jnp.sum(u * d, axis=1, keepdims=True))).astype(BF16)
 
-    for pair in range(2):
-        summed = jnp.sum(loss_acc[pair], axis=0, keepdims=True)
-        for k in range(8):
-            loss_send[8 * pair + k, :1, :rows] = summed[:, k * rows : (k + 1) * rows]
-    for k, (dp, dq) in enumerate(PLANE_SLOTS):
-        if (dp, dq) != (0, 0):
-            i = ((4 - dq) % 4) * 4 + (4 - dp) % 4
-            send(loss_send.at[k], loss_recv.at[i], l_send, l_recv, dev_b(dp, dq), keep=False)
-
+    images.run(images.first)
+    a_step(1)
+    weight(2)
+    a_step(2)
+    images.last((0, 3))
+    project(8, 13)
+    images.run(images.second)
+    a_step(3)
+    project(13, 16)
+    a_finish("0", "L1", "S1")
+    cell(2, 1)
+    images.run(images.third)
+    a_finish("L2", "S2")
+    cell(1, 1)
+    a_step(4)
+    images.last((3, 1), (1, 3), (0, 2))
+    project(0, 3)
+    a_finish("L3", "S3", "L4")
+    cell(0, 1)
     image_half(1)
+    images.last((2, 1), (3, 2), (1, 2), (2, 2))
+    project(3, 8)
+    cell(2, 0)
+    cell(1, 0)
+    cell(0, 0)
     image_half(0)
 
     block = 384
@@ -378,6 +368,15 @@
             )
     for dp in range(4):
         qo[dp] = unit(dp, 0)
+    for pair in range(2):
+        summed = jnp.sum(loss_acc[pair], axis=0, keepdims=True)
+        for k in range(8):
+            loss_send[8 * pair + k, :1, :rows] = summed[:, k * rows : (k + 1) * rows]
+    for k, (dp, dq) in enumerate(PLANE_SLOTS):
+        if (dp, dq) != (0, 0):
+            i = ((4 - dq) % 4) * 4 + (4 - dp) % 4
+            send(loss_send.at[k], loss_recv.at[i], l_send, l_recv, dev_b(dp, dq), keep=False)
+
     text_batch(1)
     ring("L4")
     text_batch(2)

time: 64.5 us -> 64.4 us (level)
  no operation moved by 1% of the time
where the time goes in v6:
time: 64.4 us; the launch traced here: 63.9 us
  Pallas kernels  62 us (96%)
  between operations  1.93 us (3%)
    pallas_call x1, Pallas kernels, local(): pl.pallas_call(kernel, out_shape=(jax.ShapeDtypeStruct((8, 128), F32), ja...  60.3 us
    pallas_call x1, Pallas kernels, local(): pl.pallas_call(results, out_shape=(jax.ShapeDtypeStruct((1, rows), F32),...  1.65 us

profile of v6, /device:TPU:1, one launch (start us, length us, event | category | flops | bytes accessed | tf_op | source)
XLA Modules:
  0.0 63.9 jit_solution(10239721108334968549)
XLA Ops:
  1.9 60.3 %shard_map.76 = (f32[8,128]{1,0:T(8,128)}, f32[48,1152]{1,0:T(8,128)}, f32[18,288]{1,0:T(8,128)}) custom-call(f32[1]{0:T(128)S(6)} %copy.8.scale_hbm, f32[1]{0:T(128)S(6)} %copy.9.shift_hbm, bf16[48,1152]{1,0:T(8,128)(2,1)} %feats_hbm.1, bf16[1152,1152]{1,0:T(8,128)(2,1)} %w_hbm.1, bf16[48,1152]{1,0:T(8,128)(2,1)} %text_hbm.1), custom_call_target="tpu_custom_call" | custom-call | tf_op jit(solution)/shard_map/pallas_call | solution.py:467
  62.2 1.6 %shard_map.77 = (f32[1,48]{1,0:T(1,128)}, f32[48,1152]{1,0:T(8,128)}, f32[18,288]{1,0:T(8,128)}) custom-call(f32[8,128]{1,0:T(8,128)} %get-tuple-element.9.loss_ref, f32[48,1152]{1,0:T(8,128)} %get-tuple-element.10.dtext_ref, f32[18,288]{1,0:T(8,128)} %get-tuple-element.11.dproj_ref), custom_call_target="tpu_custom_call" | custom-call | tf_op jit(solution)/shard_map/pallas_call | solution.py:525

commit v7 on v6

--- a/solution.py
+++ b/solution.py
@@ -223,6 +223,7 @@
     for copy in inputs[2:]:
         copy.wait()
     weight(0)
+    a_step(1)
     weight(1)
 
     half = 8 * rows
@@ -266,7 +267,6 @@
         dzb[r, :] = (inv[r, :1] * (d - u * jnp.sum(u * d, axis=1, keepdims=True))).astype(BF16)
 
     images.run(images.first)
-    a_step(1)
     weight(2)
     a_step(2)
     images.last((0, 3))

time: 64.4 us -> 63.1 us (0.980)
  Pallas kernels: 62 us -> 60.4 us
    pallas_call x1, Pallas kernels: 60.3 us -> 58.8 us  [local(): pl.pallas_call(kernel, out_shape=(jax.ShapeDtypeStruct((8, 128), F32), ja...]
where the time goes in v7:
time: 63.1 us; the launch traced here: 62.4 us
  Pallas kernels  60.4 us (96%)
  between operations  1.93 us (3%)
    pallas_call x1, Pallas kernels, local(): pl.pallas_call(kernel, out_shape=(jax.ShapeDtypeStruct((8, 128), F32), ja...  58.8 us
    pallas_call x1, Pallas kernels, local(): pl.pallas_call(results, out_shape=(jax.ShapeDtypeStruct((1, rows), F32),...  1.65 us

profile of v7, /device:TPU:1, one launch (start us, length us, event | category | flops | bytes accessed | tf_op | source)
XLA Modules:
  0.0 62.4 jit_solution(2644486527096753900)
XLA Ops:
  1.9 58.8 %shard_map.76 = (f32[8,128]{1,0:T(8,128)}, f32[48,1152]{1,0:T(8,128)}, f32[18,288]{1,0:T(8,128)}) custom-call(f32[1]{0:T(128)S(6)} %copy.8.scale_hbm, f32[1]{0:T(128)S(6)} %copy.9.shift_hbm, bf16[48,1152]{1,0:T(8,128)(2,1)} %feats_hbm.1, bf16[1152,1152]{1,0:T(8,128)(2,1)} %w_hbm.1, bf16[48,1152]{1,0:T(8,128)(2,1)} %text_hbm.1), custom_call_target="tpu_custom_call" | custom-call | tf_op jit(solution)/shard_map/pallas_call | solution.py:467
  60.7 1.6 %shard_map.77 = (f32[1,48]{1,0:T(1,128)}, f32[48,1152]{1,0:T(8,128)}, f32[18,288]{1,0:T(8,128)}) custom-call(f32[8,128]{1,0:T(8,128)} %get-tuple-element.9.loss_ref, f32[48,1152]{1,0:T(8,128)} %get-tuple-element.10.dtext_ref, f32[18,288]{1,0:T(8,128)} %get-tuple-element.11.dproj_ref), custom_call_target="tpu_custom_call" | custom-call | tf_op jit(solution)/shard_map/pallas_call | solution.py:525
